TPU v7x, 32 devices: a whole 2x2x4 slice. The times are simulated.
32 devices in a mesh: dp: 8 (over z, core), mp: 4 (over y, x).
Axes of the slice: x: 2, y: 2, z: 4, core: 2. Of those that a mesh axis runs over, the one named last changes fastest.
Arguments:
- x_in: bfloat16 [8, 1024, 2048], P('dp'), may hold values from -6 to 6
- lengths: int32 [8], P('dp'), may hold values from 512 to 1024, as said below
- gain_attn: bfloat16 [2048], P('dp'), may hold values from 0.5 to 1.5
- query_weight: bfloat16 [2048, 2048], P('dp', 'mp'), may hold values from -0.125 to 0.125
- key_projection_matrix: bfloat16 [2048, 4, 256], P('dp', None, 'mp'), may hold values from -0.125 to 0.125
- value_projection_matrix: bfloat16 [2048, 4, 256], P('dp', None, 'mp'), may hold values from -0.125 to 0.125
- out_weight: bfloat16 [2048, 2048], P('mp', 'dp'), may hold values from -0.75 to 0.75
- gain_ffn: bfloat16 [2048], P('dp'), may hold values from 0.5 to 1.5
- gate_weight: bfloat16 [2048, 8192], P('dp', 'mp'), may hold values from -0.125 to 0.125
- up_weight: bfloat16 [2048, 8192], P('dp', 'mp'), may hold values from -0.125 to 0.125
- down_weight: bfloat16 [8192, 2048], P('mp', 'dp'), may hold values from -0.0625 to 0.0625
- cotangent: bfloat16 [8, 1024, 2048], P('dp'), may hold values from -6 to 6
Outputs:
- layer_out: bfloat16 [8, 1024, 2048], P('dp')
- grad_input: float32 [8, 1024, 2048], P('dp')
- gain_attn_grad: float32 [2048], P('dp')
- query_grad: float32 [2048, 2048], P('dp', 'mp')
- key_projection_grad: float32 [2048, 4, 256], P('dp', None, 'mp')
- value_projection_grad: float32 [2048, 4, 256], P('dp', None, 'mp')
- out_grad: float32 [2048, 2048], P('mp', 'dp')
- gain_ffn_grad: float32 [2048], P('dp')
- gate_grad: float32 [2048, 8192], P('dp', 'mp')
- up_grad: float32 [2048, 8192], P('dp', 'mp')
- down_grad: float32 [8192, 2048], P('mp', 'dp')
Inputs may be any that keep to these rules, and one draw needn't show every extreme that they name: A sequence's valid slots are its first lengths positions; in every draw some sequence fills all 1024 slots.
All inputs are finite; a program needn't handle non-finite values.
Results may differ from a plain program's by a relative error of at most 0.014.
Values may be sent and summed in bfloat16 or wider, within the bound.
No kernel may reach another device: no remote copies, remote signals or barrier semaphores. Data moves between devices by JAX's collectives and lax.ppermute only.
A program may use at most 256 MiB of HBM per device.

v0:
```python
import jax
import jax.numpy as jnp
from jax import lax
from jax.sharding import PartitionSpec as P

QUERY_HEADS = 8
KEY_VALUE_HEADS = 4
HEAD_SIZE = 256
eps_norm = 1e-06
rope_base = 1000042.0
neg_large = -1e30
bf16 = jnp.bfloat16
f32 = jnp.float32


def rope_tables(slot_length, size):
    half_size = size // 2
    inv_freq = rope_base ** (-(jnp.arange(half_size, dtype=f32) * 2.0 / size))
    angles = jnp.arange(slot_length, dtype=f32)[:, None] * inv_freq[None, :]
    return (jnp.cos(angles), jnp.sin(angles))


def rotate(values, cos_b, sin_b):
    half = values.shape[-1] // 2
    a, b = (values[..., :half], values[..., half:])
    return jnp.concatenate([a * cos_b - b * sin_b, b * cos_b + a * sin_b], axis=-1)


def rotate_back(grads, cos_b, sin_b):
    half = grads.shape[-1] // 2
    a, b = (grads[..., :half], grads[..., half:])
    return jnp.concatenate([a * cos_b + b * sin_b, b * cos_b - a * sin_b], axis=-1)


def mm(left, right):
    return lax.dot_general(left, right, (((1,), (0,)), ((), ())), preferred_element_type=f32)


def mm_t(left, right):
    return lax.dot_general(left, right, (((1,), (1,)), ((), ())), preferred_element_type=f32)


def mm_rows(left, right):
    return lax.dot_general(left, right, (((0,), (0,)), ((), ())), preferred_element_type=f32)


OVER_X = [(0, 1), (1, 0), (2, 3), (3, 2)]
OVER_Y = [(0, 2), (2, 0), (1, 3), (3, 1)]


def pick(blocks, which):
    return lax.dynamic_index_in_dim(blocks, which, 0, keepdims=False)


def scatter_rows(product, lefts, width):
    mp_size = lax.axis_size("mp")
    rows = lefts[0].shape[0]
    here = rows // mp_size
    if mp_size != 4:
        part = jnp.concatenate([product(lefts, 0), product(lefts, 1)], axis=1).astype(bf16)
        return lax.psum_scatter(part, "mp", scatter_dimension=0, tiled=True).astype(f32)
    me = lax.axis_index("mp")
    x, y = (me % 2, me // 2)
    half = width // 2

    def rows_x(which):
        return [
            lax.dynamic_index_in_dim(
                v.reshape(2, 2, here, v.shape[1]), which, 1, keepdims=False
            ).reshape(2 * here, v.shape[1])
            for v in lefts
        ]

    def rows_y(which):
        return [
            lax.dynamic_index_in_dim(v.reshape(2, 2 * here, v.shape[1]), which, 0, keepdims=False)
            for v in lefts
        ]

    away_a = lax.ppermute(product(rows_x(1 - x), 0).astype(bf16), "mp", OVER_X)
    away_b = lax.ppermute(product(rows_y(1 - y), 1).astype(bf16), "mp", OVER_Y)
    sum_a = (product(rows_x(x), 0) + away_a.astype(f32)).reshape(2, here, half)
    sum_b = (product(rows_y(y), 1) + away_b.astype(f32)).reshape(2, here, half)
    last_a = lax.ppermute(pick(sum_a, 1 - y).astype(bf16), "mp", OVER_Y)
    last_b = lax.ppermute(pick(sum_b, 1 - x).astype(bf16), "mp", OVER_X)
    return jnp.concatenate(
        [pick(sum_a, y) + last_a.astype(f32), pick(sum_b, x) + last_b.astype(f32)], axis=1
    )


def gather_rows(block):
    mp_size = lax.axis_size("mp")
    if mp_size != 4:
        return lax.all_gather(block, "mp", axis=0, tiled=True)
    me = lax.axis_index("mp")
    x, y = (me % 2, me // 2)
    here, width = block.shape
    half = width // 2
    own_a, own_b = (block[:, :half], block[:, half:])

    def both(own, other, low):
        return (jnp.where(low, own, other), jnp.where(low, other, own))

    got_a = lax.ppermute(own_a, "mp", OVER_Y)
    got_b = lax.ppermute(own_b, "mp", OVER_X)
    pair_a = jnp.stack(both(own_a, got_a, y == 0))
    pair_b = jnp.stack(both(own_b, got_b, x == 0))
    far_a = lax.ppermute(pair_a, "mp", OVER_X)
    far_b = lax.ppermute(pair_b, "mp", OVER_Y)
    all_a = jnp.stack(both(pair_a, far_a, x == 0), axis=1)
    all_b = jnp.stack(both(pair_b, far_b, y == 0), axis=0)
    return jnp.concatenate([all_a.reshape(4 * here, half), all_b.reshape(4 * here, half)], axis=1)


def mask_block(first_row, block_rows, slots, seq_len):
    q_pos = first_row + jnp.arange(block_rows)
    k_pos = jnp.arange(slots)
    return (k_pos[None, :] <= q_pos[:, None]) & (k_pos[None, :] < seq_len)


def attend(queries, keys, values, seq_len, factor):
    slots = keys.shape[0]
    block_rows = min(512, slots)
    parts, totals = ([], [])
    for first_row in range(0, slots, block_rows):
        upto = first_row + block_rows
        raw = jnp.einsum(
            "qhd,kd->hqk", queries[first_row:upto], keys[:upto], preferred_element_type=f32
        )
        allowed = mask_block(first_row, block_rows, upto, seq_len)
        scores = jnp.where(allowed[None], raw * factor, neg_large)
        row_max = jnp.max(scores, axis=-1, keepdims=True)
        exps = jnp.exp(scores - row_max)
        total = jnp.sum(exps, axis=-1, keepdims=True)
        probs = (exps / total).astype(bf16)
        parts.append(
            jnp.einsum("hqk,kd->qhd", probs, values[:upto], preferred_element_type=f32).astype(bf16)
        )
        totals.append((row_max + jnp.log(total))[..., 0])
    return (jnp.concatenate(parts, axis=0), jnp.concatenate(totals, axis=1))


def attend_back(queries, keys, values, grad_ctx, log_total, seq_len, factor):
    slots = keys.shape[0]
    block_rows = min(512, slots)
    dq_parts = []
    d_keys = jnp.zeros(keys.shape, f32)
    d_values = jnp.zeros(values.shape, f32)
    for first_row in range(0, slots, block_rows):
        upto = first_row + block_rows
        q_block = queries[first_row:upto]
        g_block = grad_ctx[first_row:upto]
        raw = jnp.einsum("qhd,kd->hqk", q_block, keys[:upto], preferred_element_type=f32)
        allowed = mask_block(first_row, block_rows, upto, seq_len)
        scores = jnp.where(allowed[None], raw * factor, neg_large)
        probs = jnp.exp(scores - log_total[:, first_row:upto, None])
        grad_p = jnp.einsum("qhd,kd->hqk", g_block, values[:upto], preferred_element_type=f32)
        inner = jnp.sum(probs * grad_p, axis=-1, keepdims=True)
        grad_s = (probs * (grad_p - inner) * factor).astype(bf16)
        dq_parts.append(jnp.einsum("hqk,kd->qhd", grad_s, keys[:upto], preferred_element_type=f32))
        dk = jnp.einsum("hqk,qhd->kd", grad_s, q_block, preferred_element_type=f32)
        dv = jnp.einsum("hqk,qhd->kd", probs.astype(bf16), g_block, preferred_element_type=f32)
        d_keys = d_keys.at[:upto].add(dk)
        d_values = d_values.at[:upto].add(dv)
    return (jnp.concatenate(dq_parts, axis=0), d_keys, d_values)


def spread_heads(block):
    mp_size = lax.axis_size("mp")
    rows, heads, part = block.shape
    send = jnp.repeat(block, mp_size // heads, axis=1)
    got = lax.all_to_all(send, "mp", 1, 1, tiled=True)
    return got.reshape(rows, mp_size * part)


def collect_heads(block, heads):
    mp_size = lax.axis_size("mp")
    rows, size = block.shape
    got = lax.all_to_all(block.reshape(rows, mp_size, size // mp_size), "mp", 1, 1, tiled=True)
    got = got.reshape(rows, heads, mp_size // heads, size // mp_size)
    return jnp.sum(got.astype(f32), axis=2)


def gather_dp(block):
    return lax.all_gather(block, "dp", axis=0, tiled=True)


def reduce_dp(block):
    return lax.psum_scatter(block, "dp", scatter_dimension=0, tiled=True)


def local(
    x_in,
    lengths,
    gain_attn,
    query_weight,
    key_projection_matrix,
    value_projection_matrix,
    out_weight,
    gain_ffn,
    gate_weight,
    up_weight,
    down_weight,
    cotangent,
):
    _, slots, width = x_in.shape
    mp_size = lax.axis_size("mp")
    me = lax.axis_index("mp")
    heads_here = query_weight.shape[1] // HEAD_SIZE
    q_cols = query_weight.shape[1]
    factor = HEAD_SIZE ** (-0.5)
    here = slots // mp_size
    seq_len = lengths[0]
    cos_t, sin_t = rope_tables(slots, HEAD_SIZE)
    kv_block = jnp.concatenate(
        [spread_heads(key_projection_matrix), spread_heads(value_projection_matrix)], axis=1
    )
    gains = lax.all_gather(jnp.stack([gain_attn, gain_ffn]), "dp", axis=1, tiled=True).astype(f32)
    g_attn, g_ffn = (gains[0], gains[1])
    w_q = gather_dp(query_weight)
    w_kv = gather_dp(kv_block)
    w_o = gather_dp(out_weight.T)
    w_g = gather_dp(gate_weight)
    w_u = gather_dp(up_weight)
    w_d = gather_dp(down_weight.T)
    tok = x_in[0].astype(f32)
    r1 = lax.rsqrt(jnp.mean(tok * tok, axis=-1, keepdims=True) + eps_norm)
    h_attn = (tok * r1 * g_attn).astype(bf16)
    cos_h, sin_h = (cos_t[:, None, :], sin_t[:, None, :])
    queries = rotate(mm(h_attn, w_q).reshape(slots, heads_here, HEAD_SIZE), cos_h, sin_h).astype(
        bf16
    )
    kv_lin = mm(h_attn, w_kv)
    keys = rotate(kv_lin[:, :HEAD_SIZE], cos_t, sin_t).astype(bf16)
    values = kv_lin[:, HEAD_SIZE:].astype(bf16)
    context, log_total = attend(queries, keys, values, seq_len, factor)
    context = context.reshape(slots, q_cols)
    half = width // 2

    def product_out(lefts, which):
        return mm_t(lefts[0], w_o[which * half : (which + 1) * half])

    attn_rows = scatter_rows(product_out, [context], width)
    tok_here = lax.dynamic_slice_in_dim(x_in[0], me * here, here, 0).astype(f32)
    mid = tok_here + attn_rows
    r2 = lax.rsqrt(jnp.mean(mid * mid, axis=-1, keepdims=True) + eps_norm)
    n2 = mid * r2
    h_ffn = gather_rows((n2 * g_ffn).astype(bf16))
    gate = mm(h_ffn, w_g)
    up = mm(h_ffn, w_u)
    sig = jax.nn.sigmoid(gate)
    hidden = (gate * sig * up).astype(bf16)
    valid = (jnp.arange(slots)[:, None] < seq_len).astype(bf16)
    grad_low = cotangent[0] * valid
    down_grad = mm_rows(grad_low, hidden).astype(bf16)
    down_out = reduce_dp(down_grad)
    d_hidden = mm(grad_low, w_d)
    d_gate = (d_hidden * up * sig * (1.0 + gate * (1.0 - sig))).astype(bf16)
    d_up = (d_hidden * gate * sig).astype(bf16)

    def product_h2(lefts, which):
        cols = slice(which * half, (which + 1) * half)
        return mm_t(lefts[0], w_g[cols]) + mm_t(lefts[1], w_u[cols])

    d_h2 = scatter_rows(product_h2, [d_gate, d_up], width)
    gate_out = reduce_dp(mm_rows(h_ffn, d_gate).astype(bf16))
    up_out = reduce_dp(mm_rows(h_ffn, d_up).astype(bf16))
    gain_ffn_part = jnp.sum(d_h2 * n2, axis=0)
    e2 = d_h2 * g_ffn
    grad_here = lax.dynamic_slice_in_dim(grad_low, me * here, here, 0).astype(f32)
    g1 = grad_here + r2 * (e2 - n2 * jnp.mean(e2 * n2, axis=-1, keepdims=True))
    g1_low = gather_rows(g1.astype(bf16))

    def product_ffn(lefts, which):
        return mm_t(lefts[0], w_d[which * half : (which + 1) * half])

    ffn_rows = scatter_rows(product_ffn, [hidden], width)
    layer_out = gather_rows((mid + ffn_rows).astype(bf16))
    d_context = mm(g1_low, w_o).astype(bf16).reshape(slots, heads_here, HEAD_SIZE)
    out_out = reduce_dp(mm_rows(g1_low, context).astype(bf16))
    dq, dk, dv = attend_back(queries, keys, values, d_context, log_total, seq_len, factor)
    d_q = rotate_back(dq, cos_h, sin_h).astype(bf16).reshape(slots, q_cols)
    d_kv = jnp.concatenate([rotate_back(dk, cos_t, sin_t), dv], axis=1).astype(bf16)
    q_out = reduce_dp(mm_rows(h_attn, d_q).astype(bf16))
    kv_out = reduce_dp(mm_rows(h_attn, d_kv).astype(bf16))

    def product_h1(lefts, which):
        cols = slice(which * half, (which + 1) * half)
        return mm_t(lefts[0], w_q[cols]) + mm_t(lefts[1], w_kv[cols])

    d_h1 = scatter_rows(product_h1, [d_q, d_kv], width)
    r1_here = lax.dynamic_slice_in_dim(r1, me * here, here, 0)
    n1 = tok_here * r1_here
    gain_attn_part = jnp.sum(d_h1 * n1, axis=0)
    e1 = d_h1 * g_attn
    grad_in = g1 + r1_here * (e1 - n1 * jnp.mean(e1 * n1, axis=-1, keepdims=True))
    grad_input = gather_rows(grad_in.astype(bf16)).astype(f32)
    gain_parts = lax.psum(jnp.stack([gain_attn_part, gain_ffn_part]), ("dp", "mp"))
    rows_here = gain_attn.shape[0]
    gain_grads = lax.dynamic_slice_in_dim(
        gain_parts, lax.axis_index("dp") * rows_here, rows_here, 1
    )
    key_grad = collect_heads(kv_out[:, :HEAD_SIZE], KEY_VALUE_HEADS)
    value_grad = collect_heads(kv_out[:, HEAD_SIZE:], KEY_VALUE_HEADS)
    return (
        layer_out[None],
        grad_input[None],
        gain_grads[0],
        q_out.astype(f32),
        key_grad,
        value_grad,
        out_out.T.astype(f32),
        gain_grads[1],
        gate_out.astype(f32),
        up_out.astype(f32),
        down_out.T.astype(f32),
    )


def solution(mesh):
    return jax.shard_map(
        local,
        mesh=mesh,
        in_specs=(
            P("dp", None, None),
            P("dp"),
            P("dp"),
            P("dp", "mp"),
            P("dp", None, "mp"),
            P("dp", None, "mp"),
            P("mp", "dp"),
            P("dp"),
            P("dp", "mp"),
            P("dp", "mp"),
            P("mp", "dp"),
            P("dp", None, None),
        ),
        out_specs=(
            P("dp", None, None),
            P("dp", None, None),
            P("dp"),
            P("dp", "mp"),
            P("dp", None, "mp"),
            P("dp", None, "mp"),
            P("mp", "dp"),
            P("dp"),
            P("dp", "mp"),
            P("dp", "mp"),
            P("mp", "dp"),
        ),
        check_vma=False,
    )
```

profile of v0, /device:TPU:0, one launch (start us, length us, event | category | flops | bytes accessed | tf_op | source)
XLA Modules:
  0.0 940.7 jit_solution(466775596118007731)
XLA Ops:
  8.0 10.2 %all_to_all.20 = bf16[256,4,64]{0,2,1:T(8,128)(2,1)S(1)} all-to-all(bf16[256,4,64]{0,2,1:T(8,128)(2,1)} %param.28), channel_id=1, replica_groups=mesh['dp'=8,'mp'=4] {'mp'}, dimensions={1} | all-to-all | bytes 262144 | tf_op jit(solution)/shard_map/all_to_all | solution.py:172
  18.2 8.3 all_to_all.21
  33.7 12.0 %all_gather.21 = bf16[2,2048]{1,0:T(2,128)(2,1)S(1)} all-gather(bf16[2,256]{1,0:T(2,128)(2,1)S(1)} %pad_maximum_fusion.34), channel_id=1, replica_groups=mesh['dp'=8,'mp'=4] {'dp'}, dimensions={1}, use_global_device_ids=true | all-gather | bytes 9216 | tf_op jit(solution)/shard_map/all_gather | solution.py:218
  46.3 4.4 copy.93
  50.7 5.4 fusion.12
  56.1 17.9 %all-gather.7.cloned.1.call-done = bf16[2048,512]{0,1:T(8,128)(2,1)} async-done(((bf16[256,512]{0,1:T(8,128)(2,1)}), bf16[2048,512]{0,1:T(8,128)(2,1)}) %all-gather.7.cloned.1.call-update) | async-done | bytes 2097168 | tf_op jit(solution)/shard_map/all_gather | solution.py:185
  74.0 5.3 fusion.235
  94.3 11.2 %all-gather.11.cloned.1.call-done = bf16[2048,512]{0,1:T(8,128)(2,1)} async-done(((bf16[256,512]{0,1:T(8,128)(2,1)}), bf16[2048,512]{0,1:T(8,128)(2,1)}) %all-gather.11.cloned.1.call-update) | async-done | bytes 2097168 | tf_op jit(solution)/shard_map/all_gather | solution.py:185
  125.0 9.1 collective-permute-done.2
  137.9 7.5 collective-permute-done
  149.7 5.8 collective-permute-done.3
  167.0 9.1 collective-permute-done.4
  183.6 16.3 %collective-permute-done.7 = bf16[2,256,1024]{2,1,0:T(8,128)(2,1)S(1)} collective-permute-done((bf16[2,256,1024]{2,1,0:T(8,128)(2,1)S(1)}, bf16[2,256,1024]{2,1,0:T(8,128)(2,1)S(1)}, u32[]{:S(2)}, u32[]{:S(2)}) %collective-permute-start.7) | collective-permute-done | bytes 1048608 | tf_op jit(solution)/shard_map/ppermute | solution.py:109
  203.2 14.8 %fusion.237 = f32[1024,2048]{1,0:T(8,128)} fusion(bf16[1024,2048]{1,0:T(8,128)(2,1)} %bitcast_multiply_fusion.1, bf16[2048,2048]{0,1:T(8,128)(2,1)} %all-gather.17.cloned.1.call-done), kind=kOutput, calls=%fused_computation.365 | convolution fusion | flops 8589934592 | bytes 20971520 | tf_op jit(solution)/shard_map/dot_general | solution.py:36
  218.0 52.4 %all-gather.15.cloned.1.call-done = bf16[2048,2048]{1,0:T(8,128)(2,1)} async-done(((bf16[256,2048]{1,0:T(8,128)(2,1)}), bf16[2048,2048]{1,0:T(8,128)(2,1)}) %all-gather.15.cloned.1.call-update) | async-done | bytes 8388624 | tf_op jit(solution)/shard_map/all_gather | solution.py:185
  270.3 14.4 %fusion.223 = f32[1024,2048]{1,0:T(8,128)} fusion(bf16[2048,2048]{1,0:T(8,128)(2,1)} %all-gather.15.cloned.1.call-done, bf16[1024,1024]{1,0:T(8,128)(2,1)} %bitcast.429, bf16[1024,1024]{1,0:T(8,128)(2,1)} %bitcast.433), kind=kOutput, calls=%fused_computation.351 | convolution fusion | flops 8598323200 | bytes 20971520 | tf_op jit(solution)/shard_map/dot_general | solution.py:36
  284.8 67.6 %all-gather.13.cloned.1.call-done = bf16[2048,2048]{1,0:T(8,128)(2,1)} async-done(((bf16[256,2048]{1,0:T(8,128)(2,1)}), bf16[2048,2048]{1,0:T(8,128)(2,1)}) %all-gather.13.cloned.1.call-update) | async-done | bytes 8388624 | tf_op jit(solution)/shard_map/all_gather | solution.py:185
  352.4 21.8 %multiply_convert_fusion.1 = (bf16[1024,2048]{1,0:T(8,128)(2,1)}, bf16[1024,2048]{1,0:T(8,128)(2,1)}, bf16[1024,2048]{1,0:T(8,128)(2,1)}) fusion(f32[1024,2048]{1,0:T(8,128)} %fusion.237, f32[1024,2048]{1,0:T(8,128)} %fusion.223, bf16[2048,2048]{1,0:T(8,128)(2,1)} %all-gather.13.cloned.1.call-done, bf16[1024,1024]{1,0:T(8,128)(2,1)} %bitcast.430, ...), kind=kOutput, calls=%fused_computation.12 | convolution fusion | flops 8631877632 | bytes 41943040 | tf_op jit(solution)/shard_map/dot_general | solution.py:36
  374.2 6.3 fusion.92
  382.0 4.7 fusion.17
  399.5 5.9 fusion.25
  405.4 5.4 add_convert_fusion.3
  411.4 5.9 fusion.27
  417.3 4.5 fusion.19
  428.6 4.9 convert_add_fusion.3
  435.1 11.0 %collective-permute-done.16 = bf16[512,1024]{1,0:T(8,128)(2,1)S(1)} collective-permute-done((bf16[512,1024]{1,0:T(8,128)(2,1)S(1)}, bf16[512,1024]{1,0:T(8,128)(2,1)S(1)}, u32[]{:S(2)}, u32[]{:S(2)}) %collective-permute-start.16) | collective-permute-done | bytes 1048608 | tf_op jit(solution)/shard_map/ppermute | solution.py:80
  446.2 5.3 convert_add_fusion.4
  456.6 10.8 %collective-permute-done.19 = bf16[256,1024]{1,0:T(8,128)(2,1)S(1)} collective-permute-done((bf16[256,1024]{1,0:T(8,128)(2,1)S(1)}, bf16[256,1024]{1,0:T(8,128)(2,1)S(1)}, u32[]{:S(2)}, u32[]{:S(2)}) %collective-permute-start.19) | collective-permute-done | bytes 524320 | tf_op jit(solution)/shard_map/ppermute | solution.py:85
  468.5 5.6 collective-permute-done.9
  481.2 7.8 collective-permute-done.20
  493.5 17.6 %collective-permute-done.23 = bf16[2,256,1024]{2,1,0:T(8,128)(2,1)S(1)} collective-permute-done((bf16[2,256,1024]{2,1,0:T(8,128)(2,1)S(1)}, bf16[2,256,1024]{2,1,0:T(8,128)(2,1)S(1)}, u32[]{:S(2)}, u32[]{:S(2)}) %collective-permute-start.23) | collective-permute-done | bytes 1048608 | tf_op jit(solution)/shard_map/ppermute | solution.py:109
  531.7 9.8 %fusion.115 = f32[1024,256]{0,1:T(8,128)} fusion(f32[1024,512,2]{1,0,2:T(8,128)} %fusion.188, f32[2,512,1024]{1,2,0:T(8,128)} %copy-done.21, f32[2,512]{1,0:T(2,128)S(1)} %log_add_fusion, f32[512,256]{0,1:T(8,128)} %fusion.125, bf16[1024,2,128]{0,2,1:T(8,128)(2,1)} %copy-done.44, bf16[1024,2,128]{0,2,1:T(8,128)(2,1)} %copy-done.42), kind=kOutput, calls=%fused_computation.153 | convolution fusion | flops 545523712 | bytes 11014144 | tf_op jit(solution)/shard_map/hqk,qhd->kd/dot_general | solution.py:161
  546.4 6.2 convolution_convert_fusion.4
  553.7 5.9 convolution_convert_fusion.3
  563.4 9.6 %fusion.113 = f32[512,2,256]{0,2,1:T(8,128)} fusion(f32[1024,512,2]{1,0,2:T(8,128)} %fusion.188, f32[2,512,1024]{1,2,0:T(8,128)} %copy-done.21, f32[2,512]{1,0:T(2,128)S(1)} %log_add_fusion, bf16[1024,128]{0,1:T(8,128)(2,1)} %copy-done.45, bf16[1024,128]{0,1:T(8,128)(2,1)} %copy-done.46), kind=kOutput, calls=%fused_computation.151 | convolution fusion | flops 545261568 | bytes 9965568 | tf_op jit(solution)/shard_map/hqk,kd->qhd/dot_general | solution.py:160
  579.9 14.1 %convolution_convert_fusion = bf16[2048,2048]{1,0:T(8,128)(2,1)} fusion(bf16[1024,2048]{1,0:T(8,128)(2,1)} %bitcast_multiply_fusion.1, bf16[1024,2048]{1,0:T(8,128)(2,1)} %get-tuple-element.117), kind=kOutput, calls=%fused_computation.15 | convolution fusion | flops 8594128896 | bytes 16777216 | tf_op jit(solution)/shard_map/dot_general | solution.py:44
  595.6 13.4 %convolution_convert_fusion.2 = bf16[2048,2048]{1,0:T(8,128)(2,1)} fusion(bf16[1024,2048]{1,0:T(8,128)(2,1)} %get-tuple-element.116, bf16[1024,1024]{1,0:T(8,128)(2,1)S(1)} %bitcast.431, bf16[1024,1024]{1,0:T(8,128)(2,1)} %bitcast.435), kind=kOutput, calls=%fused_computation.17 | convolution fusion | flops 8602517504 | bytes 16777216 | tf_op jit(solution)/shard_map/dot_general | solution.py:44
  609.1 13.6 %convolution_convert_fusion.1 = bf16[2048,2048]{1,0:T(8,128)(2,1)} fusion(bf16[1024,2048]{1,0:T(8,128)(2,1)} %get-tuple-element.118, bf16[1024,1024]{1,0:T(8,128)(2,1)S(1)} %bitcast.432, bf16[1024,1024]{1,0:T(8,128)(2,1)} %bitcast.436), kind=kOutput, calls=%fused_computation.16 | convolution fusion | flops 8602517504 | bytes 16777216 | tf_op jit(solution)/shard_map/dot_general | solution.py:44
  627.1 7.3 collective-permute-done.12
  663.4 13.3 %collective-permute-done.26 = bf16[512,1024]{1,0:T(8,128)(2,1)S(1)} collective-permute-done((bf16[512,1024]{1,0:T(8,128)(2,1)S(1)}, bf16[512,1024]{1,0:T(8,128)(2,1)S(1)}, u32[]{:S(2)}, u32[]{:S(2)}) %collective-permute-start.26) | collective-permute-done | bytes 1048608 | tf_op jit(solution)/shard_map/ppermute | solution.py:81
  679.0 6.8 collective-permute-done.24
  690.6 6.5 collective-permute-done.27
  706.3 8.5 collective-permute-done.15
  720.4 6.1 collective-permute-done.30
  733.9 45.3 %psum.7 = f32[2,2048]{1,0:T(2,128)S(1)} all-reduce(f32[2,2048]{1,0:T(2,128)S(1)} %pad_maximum_fusion.33), channel_id=1, replica_groups=mesh['dp'=8,'mp'=4] {'dp','mp'}, use_global_device_ids=true, to_apply=%region_12.13 | all-reduce | flops 4096 | bytes 32768 | tf_op jit(solution)/shard_map/psum | solution.py:298
  789.8 6.0 maximum_convert_fusion
  809.8 31.0 %reduce-scatter.13.cloned.1.call-done = bf16[256,2048]{1,0:T(8,128)(2,1)} async-done(((bf16[2048,2048]{1,0:T(8,128)(2,1)}), bf16[256,2048]{1,0:T(8,128)(2,1)}) %reduce-scatter.13.cloned.1.call-update) | async-done | bytes 1048592 | tf_op jit(solution)/shard_map/reduce_scatter | solution.py:189
  843.6 87.3 %reduce-scatter.15.cloned.1.call-done = bf16[256,2048]{1,0:T(8,128)(2,1)} async-done(((bf16[2048,2048]{1,0:T(8,128)(2,1)}), bf16[256,2048]{1,0:T(8,128)(2,1)}) %reduce-scatter.15.cloned.1.call-update) | async-done | bytes 1048592 | tf_op jit(solution)/shard_map/reduce_scatter | solution.py:189
  (371 shorter events, 244.3 us)
Async XLA Ops:
  7.2 39.1 %all-gather.9.cloned.1.call-start = ((), (), s32[]{:S(2)}) async-start(), calls=%async_computation.11 | async-start | bytes 2359296 | tf_op jit(solution)/shard_map/all_gather | solution.py:185
  7.9 66.1 %all-gather.7.cloned.1.call-start = ((), (), s32[]{:S(2)}) async-start(), calls=%async_computation.10 | async-start | bytes 2359296 | tf_op jit(solution)/shard_map/all_gather | solution.py:185
  27.2 78.3 %all-gather.11.cloned.1.call-start = ((), (), s32[]{:S(2)}) async-start(), calls=%async_computation.12 | async-start | bytes 2359296 | tf_op jit(solution)/shard_map/all_gather | solution.py:185
  28.0 175.2 %all-gather.17.cloned.1.call-start = ((), (), s32[]{:S(2)}) async-start(), calls=%async_computation.15 | async-start | bytes 9437184 | tf_op jit(solution)/shard_map/all_gather | solution.py:185
  28.5 241.8 %all-gather.15.cloned.1.call-start = ((), (), s32[]{:S(2)}) async-start(), calls=%async_computation.14 | async-start | bytes 9437184 | tf_op jit(solution)/shard_map/all_gather | solution.py:185
  29.1 323.3 %all-gather.13.cloned.1.call-start = ((), (), s32[]{:S(2)}) async-start(), calls=%async_computation.13 | async-start | bytes 9437184 | tf_op jit(solution)/shard_map/all_gather | solution.py:185
  29.7 754.8 %reduce-scatter.9.cloned.1.call-start = ((), (), s32[]{:S(2)}) async-start(), calls=%async_computation.17 | async-start | bytes 2359296 | tf_op jit(solution)/shard_map/reduce_scatter | solution.py:189
  29.8 49.6 %copy-start.59 = (f32[128]{0:T(128)}, f32[128]{0:T(128)S(1)}, u32[]{:S(2)}) copy-start(f32[128]{0:T(128)S(1)} %negate_power_fusion) | copy-start | bytes 1540
  33.7 40.4 %copy-start.57 = (f32[1024]{0:T(1024)}, f32[1024]{0:T(1024)S(1)}, u32[]{:S(2)}) copy-start(f32[1024]{0:T(1024)S(1)} %add_rsqrt_fusion) | copy-start | bytes 12292
  108.5 25.6 %collective-permute-start.2 = (bf16[512,1024]{1,0:T(8,128)(2,1)}, bf16[512,1024]{1,0:T(8,128)(2,1)}, u32[]{:S(2)}, u32[]{:S(2)}) collective-permute-start(bf16[512,1024]{1,0:T(8,128)(2,1)} %convolution_convert_fusion.5), channel_id=1, source_target_pairs={{0,2},{2,0},{1,3},{3,1},{4,6},{6,4},{5,7},{7,5},{8,10},{10,8},{9,1... | collective-permute-start | bytes 3145736 | tf_op jit(solution)/shard_map/ppermute | solution.py:81
  119.0 26.4 %collective-permute-start = (bf16[512,1024]{1,0:T(8,128)(2,1)}, bf16[512,1024]{1,0:T(8,128)(2,1)}, u32[]{:S(2)}, u32[]{:S(2)}) collective-permute-start(bf16[512,1024]{1,0:T(8,128)(2,1)} %convolution_convert_fusion.6), channel_id=1, source_target_pairs={{0,1},{1,0},{2,3},{3,2},{4,5},{5,4},{6,7},{7,6},{8,9},{9,8},{10,11... | collective-permute-start | bytes 3145736 | tf_op jit(solution)/shard_map/ppermute | solution.py:80
  136.6 18.9 %collective-permute-start.3 = (bf16[256,1024]{1,0:T(8,128)(2,1)S(1)}, bf16[256,1024]{1,0:T(8,128)(2,1)}, u32[]{:S(2)}, u32[]{:S(2)}) collective-permute-start(bf16[256,1024]{1,0:T(8,128)(2,1)S(1)} %fusion.170), channel_id=1, source_target_pairs={{0,1},{1,0},{2,3},{3,2},{4,5},{5,4},{6,7},{7,6},{8,9},{9,8},{10,11... | collective-permute-start | bytes 1572872 | tf_op jit(solution)/shard_map/ppermute | solution.py:85
  148.7 12.0 %collective-permute-start.1 = (bf16[256,1024]{1,0:T(8,128)(2,1)S(1)}, bf16[256,1024]{1,0:T(8,128)(2,1)}, u32[]{:S(2)}, u32[]{:S(2)}) collective-permute-start(bf16[256,1024]{1,0:T(8,128)(2,1)S(1)} %fusion.169), channel_id=1, source_target_pairs={{0,2},{2,0},{1,3},{3,1},{4,6},{6,4},{5,7},{7,5},{8,10},{10,8},{9,1... | collective-permute-start | bytes 1572872 | tf_op jit(solution)/shard_map/ppermute | solution.py:84
  164.9 11.3 %collective-permute-start.4 = (bf16[256,1024]{1,0:T(8,128)(2,1)}, bf16[256,1024]{1,0:T(8,128)(2,1)}, u32[]{:S(2)}, u32[]{:S(2)}) collective-permute-start(bf16[256,1024]{1,0:T(8,128)(2,1)} %get-tuple-element.188), channel_id=1, source_target_pairs={{0,2},{2,0},{1,3},{3,1},{4,6},{6,4},{5,7},{7,5},{8,10},{10,8},{9,1... | collective-permute-start | bytes 1572872 | tf_op jit(solution)/shard_map/ppermute | solution.py:104
  166.0 11.2 %collective-permute-start.6 = (bf16[256,1024]{1,0:T(8,128)(2,1)}, bf16[256,1024]{1,0:T(8,128)(2,1)}, u32[]{:S(2)}, u32[]{:S(2)}) collective-permute-start(bf16[256,1024]{1,0:T(8,128)(2,1)} %get-tuple-element.189), channel_id=1, source_target_pairs={{0,1},{1,0},{2,3},{3,2},{4,5},{5,4},{6,7},{7,6},{8,9},{9,8},{10,11... | collective-permute-start | bytes 1572872 | tf_op jit(solution)/shard_map/ppermute | solution.py:105
  178.7 21.2 %collective-permute-start.7 = (bf16[2,256,1024]{2,1,0:T(8,128)(2,1)S(1)}, bf16[2,256,1024]{2,1,0:T(8,128)(2,1)S(1)}, u32[]{:S(2)}, u32[]{:S(2)}) collective-permute-start(bf16[2,256,1024]{2,1,0:T(8,128)(2,1)S(1)} %pad_maximum_fusion.19), channel_id=1, source_target_pairs={{0,2},{2,0},{1,3},{3,1},{4,6},{6,4},{5,7},{7,5},{8,10},{10,8},{9,1... | collective-permute-start | bytes 3145736 | tf_op jit(solution)/shard_map/ppermute | solution.py:109
  179.5 22.0 %collective-permute-start.5 = (bf16[2,256,1024]{2,1,0:T(8,128)(2,1)S(1)}, bf16[2,256,1024]{2,1,0:T(8,128)(2,1)S(1)}, u32[]{:S(2)}, u32[]{:S(2)}) collective-permute-start(bf16[2,256,1024]{2,1,0:T(8,128)(2,1)S(1)} %pad_maximum_fusion.18), channel_id=1, source_target_pairs={{0,1},{1,0},{2,3},{3,2},{4,5},{5,4},{6,7},{7,6},{8,9},{9,8},{10,11... | collective-permute-start | bytes 3145736 | tf_op jit(solution)/shard_map/ppermute | solution.py:108
  380.5 41.3 %collective-permute-start.10 = (bf16[512,1024]{1,0:T(8,128)(2,1)}, bf16[512,1024]{1,0:T(8,128)(2,1)}, u32[]{:S(2)}, u32[]{:S(2)}) collective-permute-start(bf16[512,1024]{1,0:T(8,128)(2,1)} %fusion.92), channel_id=1, source_target_pairs={{0,2},{2,0},{1,3},{3,1},{4,6},{6,4},{5,7},{7,5},{8,10},{10,8},{9,1... | collective-permute-start | bytes 3145736 | tf_op jit(solution)/shard_map/ppermute | solution.py:81
  390.1 38.5 %collective-permute-start.18 = (bf16[512,1024]{1,0:T(8,128)(2,1)}, bf16[512,1024]{1,0:T(8,128)(2,1)}, u32[]{:S(2)}, u32[]{:S(2)}) collective-permute-start(bf16[512,1024]{1,0:T(8,128)(2,1)} %add_convert_fusion.2), channel_id=1, source_target_pairs={{0,2},{2,0},{1,3},{3,1},{4,6},{6,4},{5,7},{7,5},{8,10},{10,8},{9,1... | collective-permute-start | bytes 3145736 | tf_op jit(solution)/shard_map/ppermute | solution.py:81
  397.4 55.7 %collective-permute-start.8 = (bf16[512,1024]{1,0:T(8,128)(2,1)}, bf16[512,1024]{1,0:T(8,128)(2,1)S(1)}, u32[]{:S(2)}, u32[]{:S(2)}) collective-permute-start(bf16[512,1024]{1,0:T(8,128)(2,1)} %fusion.98), channel_id=1, source_target_pairs={{0,1},{1,0},{2,3},{3,2},{4,5},{5,4},{6,7},{7,6},{8,9},{9,8},{10,11... | collective-permute-start | bytes 3145736 | tf_op jit(solution)/shard_map/ppermute | solution.py:80
  410.8 35.4 %collective-permute-start.16 = (bf16[512,1024]{1,0:T(8,128)(2,1)S(1)}, bf16[512,1024]{1,0:T(8,128)(2,1)S(1)}, u32[]{:S(2)}, u32[]{:S(2)}) collective-permute-start(bf16[512,1024]{1,0:T(8,128)(2,1)S(1)} %add_convert_fusion.3), channel_id=1, source_target_pairs={{0,1},{1,0},{2,3},{3,2},{4,5},{5,4},{6,7},{7,6},{8,9},{9,8},{10,11... | collective-permute-start | bytes 3145736 | tf_op jit(solution)/shard_map/ppermute | solution.py:80
  425.5 42.9 %collective-permute-start.11 = (bf16[256,1024]{1,0:T(8,128)(2,1)S(1)}, bf16[256,1024]{1,0:T(8,128)(2,1)S(1)}, u32[]{:S(2)}, u32[]{:S(2)}) collective-permute-start(bf16[256,1024]{1,0:T(8,128)(2,1)S(1)} %fusion.172), channel_id=1, source_target_pairs={{0,1},{1,0},{2,3},{3,2},{4,5},{5,4},{6,7},{7,6},{8,9},{9,8},{10,11... | collective-permute-start | bytes 1572872 | tf_op jit(solution)/shard_map/ppermute | solution.py:85
  433.6 33.8 %collective-permute-start.19 = (bf16[256,1024]{1,0:T(8,128)(2,1)S(1)}, bf16[256,1024]{1,0:T(8,128)(2,1)S(1)}, u32[]{:S(2)}, u32[]{:S(2)}) collective-permute-start(bf16[256,1024]{1,0:T(8,128)(2,1)S(1)} %fusion.174), channel_id=1, source_target_pairs={{0,1},{1,0},{2,3},{3,2},{4,5},{5,4},{6,7},{7,6},{8,9},{9,8},{10,11... | collective-permute-start | bytes 1572872 | tf_op jit(solution)/shard_map/ppermute | solution.py:85
  451.5 15.9 %collective-permute-start.17 = (bf16[256,1024]{1,0:T(8,128)(2,1)S(1)}, bf16[256,1024]{1,0:T(8,128)(2,1)S(1)}, u32[]{:S(2)}, u32[]{:S(2)}) collective-permute-start(bf16[256,1024]{1,0:T(8,128)(2,1)S(1)} %fusion.173), channel_id=1, source_target_pairs={{0,2},{2,0},{1,3},{3,1},{4,6},{6,4},{5,7},{7,5},{8,10},{10,8},{9,1... | collective-permute-start | bytes 1572872 | tf_op jit(solution)/shard_map/ppermute | solution.py:84
  456.0 18.2 %collective-permute-start.9 = (bf16[256,1024]{1,0:T(8,128)(2,1)S(1)}, bf16[256,1024]{1,0:T(8,128)(2,1)S(1)}, u32[]{:S(2)}, u32[]{:S(2)}) collective-permute-start(bf16[256,1024]{1,0:T(8,128)(2,1)S(1)} %fusion.171), channel_id=1, source_target_pairs={{0,2},{2,0},{1,3},{3,1},{4,6},{6,4},{5,7},{7,5},{8,10},{10,8},{9,1... | collective-permute-start | bytes 1572872 | tf_op jit(solution)/shard_map/ppermute | solution.py:84
  478.2 10.8 %collective-permute-start.20 = (bf16[256,1024]{1,0:T(8,128)(2,1)S(1)}, bf16[256,1024]{1,0:T(8,128)(2,1)S(1)}, u32[]{:S(2)}, u32[]{:S(2)}) collective-permute-start(bf16[256,1024]{1,0:T(8,128)(2,1)S(1)} %get-tuple-element.180), channel_id=1, source_target_pairs={{0,2},{2,0},{1,3},{3,1},{4,6},{6,4},{5,7},{7,5},{8,10},{10,8},{9,1... | collective-permute-start | bytes 1572872 | tf_op jit(solution)/shard_map/ppermute | solution.py:104
  479.8 11.3 %collective-permute-start.22 = (bf16[256,1024]{1,0:T(8,128)(2,1)S(1)}, bf16[256,1024]{1,0:T(8,128)(2,1)S(1)}, u32[]{:S(2)}, u32[]{:S(2)}) collective-permute-start(bf16[256,1024]{1,0:T(8,128)(2,1)S(1)} %get-tuple-element.181), channel_id=1, source_target_pairs={{0,1},{1,0},{2,3},{3,2},{4,5},{5,4},{6,7},{7,6},{8,9},{9,8},{10,11... | collective-permute-start | bytes 1572872 | tf_op jit(solution)/shard_map/ppermute | solution.py:105
  491.3 19.8 %collective-permute-start.23 = (bf16[2,256,1024]{2,1,0:T(8,128)(2,1)S(1)}, bf16[2,256,1024]{2,1,0:T(8,128)(2,1)S(1)}, u32[]{:S(2)}, u32[]{:S(2)}) collective-permute-start(bf16[2,256,1024]{2,1,0:T(8,128)(2,1)S(1)} %pad_maximum_fusion.23), channel_id=1, source_target_pairs={{0,2},{2,0},{1,3},{3,1},{4,6},{6,4},{5,7},{7,5},{8,10},{10,8},{9,1... | collective-permute-start | bytes 3145736 | tf_op jit(solution)/shard_map/ppermute | solution.py:109
  491.9 20.4 %collective-permute-start.21 = (bf16[2,256,1024]{2,1,0:T(8,128)(2,1)S(1)}, bf16[2,256,1024]{2,1,0:T(8,128)(2,1)S(1)}, u32[]{:S(2)}, u32[]{:S(2)}) collective-permute-start(bf16[2,256,1024]{2,1,0:T(8,128)(2,1)S(1)} %pad_maximum_fusion.22), channel_id=1, source_target_pairs={{0,1},{1,0},{2,3},{3,2},{4,5},{5,4},{6,7},{7,6},{8,9},{9,8},{10,11... | collective-permute-start | bytes 3145736 | tf_op jit(solution)/shard_map/ppermute | solution.py:108
  552.5 248.2 %reduce-scatter.11.cloned.1.call-start = ((), (), s32[]{:S(2)}) async-start(), calls=%async_computation.18 | async-start | bytes 2359296 | tf_op jit(solution)/shard_map/reduce_scatter | solution.py:189
  559.7 243.1 %reduce-scatter.7.cloned.1.call-start = ((), (), s32[]{:S(2)}) async-start(), calls=%async_computation.16 | async-start | bytes 2359296 | tf_op jit(solution)/shard_map/reduce_scatter | solution.py:189
  579.8 226.7 %reduce-scatter.17.cloned.1.call-start = ((), (), s32[]{:S(2)}) async-start(), calls=%async_computation.21 | async-start | bytes 9437184 | tf_op jit(solution)/shard_map/reduce_scatter | solution.py:189
  594.0 246.8 %reduce-scatter.13.cloned.1.call-start = ((), (), s32[]{:S(2)}) async-start(), calls=%async_computation.19 | async-start | bytes 9437184 | tf_op jit(solution)/shard_map/reduce_scatter | solution.py:189
  609.0 321.8 %reduce-scatter.15.cloned.1.call-start = ((), (), s32[]{:S(2)}) async-start(), calls=%async_computation.20 | async-start | bytes 9437184 | tf_op jit(solution)/shard_map/reduce_scatter | solution.py:189
  624.9 9.4 collective-permute-start.12
  625.5 9.4 collective-permute-start.14
  657.2 19.5 %collective-permute-start.26 = (bf16[512,1024]{1,0:T(8,128)(2,1)S(1)}, bf16[512,1024]{1,0:T(8,128)(2,1)S(1)}, u32[]{:S(2)}, u32[]{:S(2)}) collective-permute-start(bf16[512,1024]{1,0:T(8,128)(2,1)S(1)} %add_convert_fusion), channel_id=1, source_target_pairs={{0,2},{2,0},{1,3},{3,1},{4,6},{6,4},{5,7},{7,5},{8,10},{10,8},{9,1... | collective-permute-start | bytes 3145736 | tf_op jit(solution)/shard_map/ppermute | solution.py:81
  660.5 25.4 %collective-permute-start.24 = (bf16[512,1024]{1,0:T(8,128)(2,1)S(1)}, bf16[512,1024]{1,0:T(8,128)(2,1)S(1)}, u32[]{:S(2)}, u32[]{:S(2)}) collective-permute-start(bf16[512,1024]{1,0:T(8,128)(2,1)S(1)} %add_convert_fusion.1), channel_id=1, source_target_pairs={{0,1},{1,0},{2,3},{3,2},{4,5},{5,4},{6,7},{7,6},{8,9},{9,8},{10,11... | collective-permute-start | bytes 3145736 | tf_op jit(solution)/shard_map/ppermute | solution.py:80
  677.6 19.5 %collective-permute-start.27 = (bf16[256,1024]{1,0:T(8,128)(2,1)S(1)}, bf16[256,1024]{1,0:T(8,128)(2,1)S(1)}, u32[]{:S(2)}, u32[]{:S(2)}) collective-permute-start(bf16[256,1024]{1,0:T(8,128)(2,1)S(1)} %fusion.176), channel_id=1, source_target_pairs={{0,1},{1,0},{2,3},{3,2},{4,5},{5,4},{6,7},{7,6},{8,9},{9,8},{10,11... | collective-permute-start | bytes 1572872 | tf_op jit(solution)/shard_map/ppermute | solution.py:85
  686.7 14.9 %collective-permute-start.25 = (bf16[256,1024]{1,0:T(8,128)(2,1)S(1)}, bf16[256,1024]{1,0:T(8,128)(2,1)S(1)}, u32[]{:S(2)}, u32[]{:S(2)}) collective-permute-start(bf16[256,1024]{1,0:T(8,128)(2,1)S(1)} %fusion.175), channel_id=1, source_target_pairs={{0,2},{2,0},{1,3},{3,1},{4,6},{6,4},{5,7},{7,5},{8,10},{10,8},{9,1... | collective-permute-start | bytes 1572872 | tf_op jit(solution)/shard_map/ppermute | solution.py:84
  687.6 27.2 %collective-permute-start.15 = (bf16[2,256,1024]{2,1,0:T(8,128)(2,1)S(1)}, bf16[2,256,1024]{2,1,0:T(8,128)(2,1)S(1)}, u32[]{:S(2)}, u32[]{:S(2)}) collective-permute-start(bf16[2,256,1024]{2,1,0:T(8,128)(2,1)S(1)} %pad_maximum_fusion.21), channel_id=1, source_target_pairs={{0,2},{2,0},{1,3},{3,1},{4,6},{6,4},{5,7},{7,5},{8,10},{10,8},{9,1... | collective-permute-start | bytes 3145736 | tf_op jit(solution)/shard_map/ppermute | solution.py:109
  689.1 28.8 %collective-permute-start.13 = (bf16[2,256,1024]{2,1,0:T(8,128)(2,1)S(1)}, bf16[2,256,1024]{2,1,0:T(8,128)(2,1)S(1)}, u32[]{:S(2)}, u32[]{:S(2)}) collective-permute-start(bf16[2,256,1024]{2,1,0:T(8,128)(2,1)S(1)} %pad_maximum_fusion.20), channel_id=1, source_target_pairs={{0,1},{1,0},{2,3},{3,2},{4,5},{5,4},{6,7},{7,6},{8,9},{9,8},{10,11... | collective-permute-start | bytes 3145736 | tf_op jit(solution)/shard_map/ppermute | solution.py:108
  704.1 16.3 %collective-permute-start.28 = (bf16[256,1024]{1,0:T(8,128)(2,1)S(1)}, bf16[256,1024]{1,0:T(8,128)(2,1)S(1)}, u32[]{:S(2)}, u32[]{:S(2)}) collective-permute-start(bf16[256,1024]{1,0:T(8,128)(2,1)S(1)} %get-tuple-element.168), channel_id=1, source_target_pairs={{0,2},{2,0},{1,3},{3,1},{4,6},{6,4},{5,7},{7,5},{8,10},{10,8},{9,1... | collective-permute-start | bytes 1572872 | tf_op jit(solution)/shard_map/ppermute | solution.py:104
  704.9 21.6 %collective-permute-start.30 = (bf16[256,1024]{1,0:T(8,128)(2,1)S(1)}, bf16[256,1024]{1,0:T(8,128)(2,1)S(1)}, u32[]{:S(2)}, u32[]{:S(2)}) collective-permute-start(bf16[256,1024]{1,0:T(8,128)(2,1)S(1)} %get-tuple-element.169), channel_id=1, source_target_pairs={{0,1},{1,0},{2,3},{3,2},{4,5},{5,4},{6,7},{7,6},{8,9},{9,8},{10,11... | collective-permute-start | bytes 1572872 | tf_op jit(solution)/shard_map/ppermute | solution.py:105
  727.7 52.1 %collective-permute-start.29 = (bf16[2,256,1024]{2,1,0:T(8,128)(2,1)}, bf16[2,256,1024]{2,1,0:T(8,128)(2,1)}, u32[]{:S(2)}, u32[]{:S(2)}) collective-permute-start(bf16[2,256,1024]{2,1,0:T(8,128)(2,1)} %pad_maximum_fusion.26), channel_id=1, source_target_pairs={{0,1},{1,0},{2,3},{3,2},{4,5},{5,4},{6,7},{7,6},{8,9},{9,8},{10,11... | collective-permute-start | bytes 3145736 | tf_op jit(solution)/shard_map/ppermute | solution.py:108
  730.9 50.8 %collective-permute-start.31 = (bf16[2,256,1024]{2,1,0:T(8,128)(2,1)}, bf16[2,256,1024]{2,1,0:T(8,128)(2,1)}, u32[]{:S(2)}, u32[]{:S(2)}) collective-permute-start(bf16[2,256,1024]{2,1,0:T(8,128)(2,1)} %pad_maximum_fusion.27), channel_id=1, source_target_pairs={{0,2},{2,0},{1,3},{3,1},{4,6},{6,4},{5,7},{7,5},{8,10},{10,8},{9,1... | collective-permute-start | bytes 3145736 | tf_op jit(solution)/shard_map/ppermute | solution.py:109
  786.3 10.3 %all-to-all-start.3 = ((bf16[256,4,64]{0,2,1:T(8,128)(2,1)}), bf16[256,4,64]{0,2,1:T(8,128)(2,1)S(1)}, u32[]{:S(2)}, u32[]{:S(2)}) async-start(bf16[256,4,64]{0,2,1:T(8,128)(2,1)} %bitcast.144), calls=%async_computation.5 | async-start | bytes 262144 | tf_op jit(solution)/shard_map/all_to_all | solution.py:179
  796.6 9.2 all-to-all-start.2
  (65 other events, 311.7 us)
Sparse Core Ops, SparseCore 0:
  9.6 31.8 all-gather.8
  43.6 30.3 all-gather.6
  75.6 29.8 all-gather.10
  107.0 81.5 all-gather.16
  190.1 80.2 all-gather.14
  271.8 80.5 all-gather.12
  552.7 33.2 reduce-scatter.8
  588.3 34.4 reduce-scatter.10
  625.1 34.3 reduce-scatter.6
  661.6 88.2 reduce-scatter.16
  752.2 88.5 reduce-scatter.12
  843.0 87.8 reduce-scatter.14
where the time goes:
time: 945 us; the launch traced here: 941 us
  waiting for transfers between devices  440 us (47%)
  matrix products  233 us (25%)
  blocking collectives  75.8 us (8%)
  local copies, waits for them, and re-layouts  65.4 us (7%)
  other arithmetic  63.3 us (7%)
  starting transfers between devices  47 us (5%)
  between operations  16.5 us (2%)
    all_gather x6, waiting for transfers between devices, gather_dp(): return lax.all_gather(block, 'dp', axis=0, tiled=True)  149 us
    reduce_scatter x6, waiting for transfers between devices, reduce_dp(): return lax.psum_scatter(block, 'dp', scatter_dimension=0, tiled=True)  118 us
    dot_general x24, matrix products, mm_t(): lax.dot_general(left, right, (((1,), (1,)), ((), ())), preferred_element_...  71.9 us
    dot_general x6, matrix products, mm(): lax.dot_general(left, right, (((1,), (0,)), ((), ())), preferred_element_...  64.1 us
    dot_general x6, matrix products, mm_rows(): lax.dot_general(left, right, (((0,), (0,)), ((), ())), preferred_element_...  57.4 us
    psum x1, blocking collectives, local(): lax.psum(jnp.stack([gain_attn_part, gain_ffn_part]), ('dp', 'mp'))  45.3 us
    ppermute x4, waiting for transfers between devices, gather_rows(): far_b = lax.ppermute(pair_b, 'mp', OVER_Y)  42.4 us
    unnamed x144, local copies, waits for them, and re-layouts  37.5 us
  transfers between devices with their start and end apart: 46, of which 32 were waited for; matrix products, arithmetic and copies ran while one was open for 29% of the time, Pallas kernels for 0%

commit v1 on v0

--- a/solution.py
+++ b/solution.py
@@ -1,3 +1,4 @@
+import functools
 import jax
 import jax.numpy as jnp
 from jax import lax
@@ -11,6 +12,32 @@
 neg_large = -1e30
 bf16 = jnp.bfloat16
 f32 = jnp.float32
+
+
+def prepare_edge(unit, along_axis):
+    e_next, later, carry = (lax.axis_size(along_axis), lax.axis_index(along_axis), unit.shape[0])
+    nodes = [(t, (t + 1) % e_next) for t in range(e_next)]
+    found_now = jnp.zeros((*unit.shape[:0], e_next * carry, *unit.shape[1:]), unit.dtype)
+    found_now = lax.dynamic_update_slice_in_dim(found_now, unit, later * carry, axis=0)
+    z_new = new = unit
+    cards = [(t, (t - 1) % e_next) for t in range(e_next)]
+    u_next = e_next // 2
+    dev = 1
+    while dev < u_next + 1:
+        z_new = lax.ppermute(z_new, along_axis, nodes)
+        found_now = lax.dynamic_update_slice_in_dim(
+            found_now, z_new, (later - dev) % e_next * carry, axis=0
+        )
+        if dev < e_next - u_next:
+            new = lax.ppermute(new, along_axis, cards)
+            found_now = lax.dynamic_update_slice_in_dim(
+                found_now, new, (later + dev) % e_next * carry, axis=0
+            )
+        dev = dev + 1
+    return found_now
+
+
+_apply_shapes = functools.partial(prepare_edge, along_axis="dp")
 
 
 def rope_tables(slot_length, size):
@@ -182,7 +209,7 @@
 
 
 def gather_dp(block):
-    return lax.all_gather(block, "dp", axis=0, tiled=True)
+    return _apply_shapes(block)
 
 
 def reduce_dp(block):

time: 945 us -> 1010 us (1.069)
  waiting for transfers between devices: 440 us -> 314 us
  local copies, waits for them, and re-layouts: 65.4 us -> 172 us
  starting transfers between devices: 47 us -> 124 us
    all_gather x6 -> x0, waiting for transfers between devices: 149 us -> none  [gather_dp(): return lax.all_gather(block, 'dp', axis=0, tiled=True)]
    ppermute x0 -> x42, waiting for transfers between devices: none -> 93.4 us  [the longest x24 90.6 us: prepare_edge(): z_new = lax.ppermute(z_new, along_axis, nodes)]
    ppermute x0 -> x42, starting transfers between devices: none -> 74.6 us  [the longest x18 62.7 us: prepare_edge(): new = lax.ppermute(new, along_axis, cards)]
    dynamic_update_slice x0 -> x47, local copies, waits for them, and re-layouts: none -> 55.6 us  [the longest x24 27.2 us: prepare_edge(): lax.dynamic_update_slice_in_dim(found_now, z_new, (later - dev) % e_next...]
    ppermute x4, waiting for transfers between devices: 42.4 us -> 1.21 us  [gather_rows(): far_b = lax.ppermute(pair_b, 'mp', OVER_Y)]
    ppermute x0 -> x21, local copies, waits for them, and re-layouts: none -> 33.6 us  [the longest x12 18.3 us: prepare_edge(): z_new = lax.ppermute(z_new, along_axis, nodes)]
    ppermute x4, waiting for transfers between devices: 25.3 us -> 0.01 us  [scatter_rows(): away_a = lax.ppermute(product(rows_x(1 - x), 0).astype(bf16), 'mp', OVER_X)]
    ppermute x4, waiting for transfers between devices: 4.18 us -> 24.3 us  [gather_rows(): far_a = lax.ppermute(pair_a, 'mp', OVER_X)]
  transfers between devices with their start and end apart: 46 -> 84, of which waited for: 32 -> 24; matrix products, arithmetic and copies ran while one was open for 29% -> 37% of each run, Pallas kernels for 0% -> 0%
where the time goes in v1:
time: 1010 us; the launch traced here: 1000 us
  waiting for transfers between devices  314 us (31%)
  matrix products  232 us (23%)
  local copies, waits for them, and re-layouts  172 us (17%)
  starting transfers between devices  124 us (12%)
  other arithmetic  72.9 us (7%)
  blocking collectives  68.3 us (7%)
  between operations  17.1 us (2%)
    reduce_scatter x6, waiting for transfers between devices, reduce_dp(): return lax.psum_scatter(block, 'dp', scatter_dimension=0, tiled=True)  100 us
    ppermute x24, waiting for transfers between devices, prepare_edge(): z_new = lax.ppermute(z_new, along_axis, nodes)  90.6 us
    dot_general x24, matrix products, mm_t(): lax.dot_general(left, right, (((1,), (1,)), ((), ())), preferred_element_...  76.3 us
    ppermute x18, starting transfers between devices, prepare_edge(): new = lax.ppermute(new, along_axis, cards)  62.7 us
    psum x1, blocking collectives, local(): lax.psum(jnp.stack([gain_attn_part, gain_ffn_part]), ('dp', 'mp'))  59.9 us
    dot_general x6, matrix products, mm_rows(): lax.dot_general(left, right, (((0,), (0,)), ((), ())), preferred_element_...  56.7 us
    dot_general x6, matrix products, mm(): lax.dot_general(left, right, (((1,), (0,)), ((), ())), preferred_element_...  56.6 us
    unnamed x203, local copies, waits for them, and re-layouts  41.3 us
  transfers between devices with their start and end apart: 84, of which 24 were waited for; matrix products, arithmetic and copies ran while one was open for 37% of the time, Pallas kernels for 0%

profile of v1, /device:TPU:0, one launch (start us, length us, event | category | flops | bytes accessed | tf_op | source)
XLA Modules:
  0.0 999.8 jit_solution(5895622164575886406)
XLA Ops:
  7.7 4.1 collective-permute-start.8
  15.3 4.2 all-to-all-start
  21.9 8.4 all_gather.3
  51.0 4.5 broadcast.266.clone.2
  58.8 4.2 all-to-all-start.1
  63.2 4.8 all-to-all-done.1
  123.3 39.4 %collective-permute-done.13 = bf16[256,512]{1,0:T(8,128)(2,1)S(1)} collective-permute-done((bf16[256,512]{1,0:T(8,128)(2,1)}, bf16[256,512]{1,0:T(8,128)(2,1)S(1)}, u32[]{:S(2)}, u32[]{:S(2)}) %collective-permute-start.13) | collective-permute-done | bytes 262176 | tf_op jit(solution)/shard_map/ppermute | solution.py:27
  163.6 6.6 fusion.12
  175.3 11.0 %collective-permute-start.20 = (bf16[256,512]{0,1:T(8,128)(2,1)}, bf16[256,512]{0,1:T(8,128)(2,1)}, u32[]{:S(2)}, u32[]{:S(2)}) collective-permute-start(bf16[256,512]{0,1:T(8,128)(2,1)} %copy-done.66), channel_id=1, source_target_pairs={{0,4},{4,8},{8,12},{12,16},{16,20},{20,24},{24,28},{28,0},{1,5},{5... | collective-permute-start | bytes 786440 | tf_op jit(solution)/shard_map/ppermute | solution.py:27
  267.8 5.1 collective-permute-done.23
  284.9 5.8 collective-permute-start.34
  304.9 33.8 %collective-permute-done.33 = bf16[256,2048]{1,0:T(8,128)(2,1)} collective-permute-done((bf16[256,2048]{1,0:T(8,128)(2,1)}, bf16[256,2048]{1,0:T(8,128)(2,1)}, u32[]{:S(2)}, u32[]{:S(2)}) %collective-permute-start.33) | collective-permute-done | bytes 1048608 | tf_op jit(solution)/shard_map/ppermute | solution.py:27
  358.7 17.3 %collective-permute-done.49 = bf16[256,2048]{0,1:T(8,128)(2,1)S(1)} collective-permute-done((bf16[256,2048]{0,1:T(8,128)(2,1)}, bf16[256,2048]{0,1:T(8,128)(2,1)S(1)}, u32[]{:S(2)}, u32[]{:S(2)}) %collective-permute-start.49) | collective-permute-done | bytes 1048608 | tf_op jit(solution)/shard_map/ppermute | solution.py:27
  376.2 11.2 %fusion.229 = f32[1024,2048]{1,0:T(8,128)} fusion(bf16[1024,2048]{1,0:T(8,128)(2,1)S(1)} %copy-done.16, bf16[2048,2048]{0,1:T(8,128)(2,1)S(1)} %constant_dynamic-update-slice_fusion), kind=kOutput, calls=%fused_computation.413 | convolution fusion | flops 8589934592 | bytes 20971520 | tf_op jit(solution)/shard_map/dot_general | solution.py:63
  400.7 11.0 %fusion.215 = f32[1024,2048]{1,0:T(8,128)} fusion(bf16[2048,2048]{0,1:T(8,128)(2,1)S(1)} %bitcast.394, bf16[1024,1024]{1,0:T(8,128)(2,1)S(1)} %bitcast.443, bf16[1024,1024]{1,0:T(8,128)(2,1)S(1)} %bitcast.439), kind=kOutput, calls=%fused_computation.399 | convolution fusion | flops 8598323200 | bytes 20971520 | tf_op jit(solution)/shard_map/dot_general | solution.py:63
  411.7 21.2 %multiply_convert_fusion.1 = (bf16[1024,2048]{1,0:T(8,128)(2,1)}, bf16[1024,2048]{1,0:T(8,128)(2,1)}, bf16[1024,2048]{1,0:T(8,128)(2,1)}) fusion(f32[1024,2048]{1,0:T(8,128)} %fusion.229, f32[1024,2048]{1,0:T(8,128)} %fusion.215, bf16[2048,2048]{0,1:T(8,128)(2,1)} %constant_dynamic-update-slice_fusion.16, bf16[1024,1024]{1,0:T(8,128)(2,1)} %bitcast.444, ...), kind=kOutput, calls=%fused_computation.12 | convolution fusion | flops 8631877632 | bytes 41943040 | tf_op jit(solution)/shard_map/dot_general | solution.py:63
  433.0 5.3 fusion.19
  438.3 6.1 fusion.17
  455.8 4.1 fusion.27
  462.5 4.1 fusion.25
  466.7 4.9 add_convert_fusion.3
  472.9 4.6 add_convert_fusion.2
  477.5 4.7 fusion.23
  482.2 4.6 fusion.31
  494.7 16.0 %collective-permute-done.60 = bf16[512,1024]{1,0:T(8,128)(2,1)S(1)} collective-permute-done((bf16[512,1024]{1,0:T(8,128)(2,1)S(1)}, bf16[512,1024]{1,0:T(8,128)(2,1)S(1)}, u32[]{:S(2)}, u32[]{:S(2)}) %collective-permute-start.60) | collective-permute-done | bytes 1048608 | tf_op jit(solution)/shard_map/ppermute | solution.py:108
  516.1 11.1 %collective-permute-done.59 = bf16[256,1024]{1,0:T(8,128)(2,1)S(1)} collective-permute-done((bf16[256,1024]{1,0:T(8,128)(2,1)S(1)}, bf16[256,1024]{1,0:T(8,128)(2,1)S(1)}, u32[]{:S(2)}, u32[]{:S(2)}) %collective-permute-start.59) | collective-permute-done | bytes 524320 | tf_op jit(solution)/shard_map/ppermute | solution.py:111
  537.3 11.8 %collective-permute-done.62 = bf16[256,1024]{1,0:T(8,128)(2,1)S(1)} collective-permute-done((bf16[256,1024]{1,0:T(8,128)(2,1)S(1)}, bf16[256,1024]{1,0:T(8,128)(2,1)S(1)}, u32[]{:S(2)}, u32[]{:S(2)}) %collective-permute-start.62) | collective-permute-done | bytes 524320 | tf_op jit(solution)/shard_map/ppermute | solution.py:131
  552.2 12.0 %collective-permute-done.63 = bf16[2,256,1024]{2,1,0:T(8,128)(2,1)S(1)} collective-permute-done((bf16[2,256,1024]{2,1,0:T(8,128)(2,1)S(1)}, bf16[2,256,1024]{2,1,0:T(8,128)(2,1)S(1)}, u32[]{:S(2)}, u32[]{:S(2)}) %collective-permute-start.63) | collective-permute-done | bytes 1048608 | tf_op jit(solution)/shard_map/ppermute | solution.py:135
  567.4 4.0 fusion.97
  576.3 4.3 fusion.121
  584.6 8.7 fusion.111
  605.3 6.0 convolution_convert_fusion.3
  612.3 5.8 fusion.105
  618.1 9.4 fusion.109
  630.8 4.2 fusion.42
  635.0 14.1 %convolution_convert_fusion = bf16[2048,2048]{1,0:T(8,128)(2,1)} fusion(bf16[1024,2048]{1,0:T(8,128)(2,1)} %bitcast_multiply_fusion.1, bf16[1024,2048]{1,0:T(8,128)(2,1)} %get-tuple-element.117), kind=kOutput, calls=%fused_computation.15 | convolution fusion | flops 8594128896 | bytes 16777216 | tf_op jit(solution)/shard_map/dot_general | solution.py:71
  649.6 14.2 %convolution_convert_fusion.1 = bf16[2048,2048]{1,0:T(8,128)(2,1)} fusion(bf16[1024,2048]{1,0:T(8,128)(2,1)} %get-tuple-element.118, bf16[1024,1024]{1,0:T(8,128)(2,1)} %bitcast.445, bf16[1024,1024]{1,0:T(8,128)(2,1)} %bitcast.441), kind=kOutput, calls=%fused_computation.16 | convolution fusion | flops 8602517504 | bytes 16777216 | tf_op jit(solution)/shard_map/dot_general | solution.py:71
  663.9 14.2 %convolution_convert_fusion.2 = bf16[2048,2048]{1,0:T(8,128)(2,1)} fusion(bf16[1024,2048]{1,0:T(8,128)(2,1)} %get-tuple-element.116, bf16[1024,1024]{1,0:T(8,128)(2,1)} %bitcast.446, bf16[1024,1024]{1,0:T(8,128)(2,1)} %bitcast.442), kind=kOutput, calls=%fused_computation.17 | convolution fusion | flops 8602517504 | bytes 16777216 | tf_op jit(solution)/shard_map/dot_general | solution.py:71
  680.9 6.6 collective-permute-done.54
  733.5 16.6 %collective-permute-done.68 = bf16[512,1024]{1,0:T(8,128)(2,1)S(1)} collective-permute-done((bf16[512,1024]{1,0:T(8,128)(2,1)}, bf16[512,1024]{1,0:T(8,128)(2,1)S(1)}, u32[]{:S(2)}, u32[]{:S(2)}) %collective-permute-start.68) | collective-permute-done | bytes 1048608 | tf_op jit(solution)/shard_map/ppermute | solution.py:108
  755.7 4.6 collective-permute-done.67
  766.2 12.3 %collective-permute-done.55 = bf16[2,256,1024]{2,1,0:T(8,128)(2,1)} collective-permute-done((bf16[2,256,1024]{2,1,0:T(8,128)(2,1)}, bf16[2,256,1024]{2,1,0:T(8,128)(2,1)}, u32[]{:S(2)}, u32[]{:S(2)}) %collective-permute-start.55) | collective-permute-done | bytes 1048608 | tf_op jit(solution)/shard_map/ppermute | solution.py:135
  780.3 7.8 collective-permute-done.70
  797.5 59.9 %psum.7 = f32[2,2048]{1,0:T(2,128)S(1)} all-reduce(f32[2,2048]{1,0:T(2,128)S(1)} %pad_maximum_fusion.33), channel_id=1, replica_groups=mesh['dp'=8,'mp'=4] {'dp','mp'}, use_global_device_ids=true, to_apply=%region_12.13 | all-reduce | flops 4096 | bytes 32768 | tf_op jit(solution)/shard_map/psum | solution.py:325
  866.8 6.0 maximum_convert_fusion
  873.5 4.2 all-to-all-start.3
  886.7 13.1 %reduce-scatter.15.cloned.1.call-done = bf16[256,2048]{1,0:T(8,128)(2,1)} async-done(((bf16[2048,2048]{1,0:T(8,128)(2,1)}), bf16[256,2048]{1,0:T(8,128)(2,1)}) %reduce-scatter.15.cloned.1.call-update) | async-done | bytes 1048592 | tf_op jit(solution)/shard_map/reduce_scatter | solution.py:216
  902.6 87.3 %reduce-scatter.13.cloned.1.call-done = bf16[256,2048]{1,0:T(8,128)(2,1)} async-done(((bf16[2048,2048]{1,0:T(8,128)(2,1)}), bf16[256,2048]{1,0:T(8,128)(2,1)}) %reduce-scatter.13.cloned.1.call-update) | async-done | bytes 1048592 | tf_op jit(solution)/shard_map/reduce_scatter | solution.py:216
  (575 shorter events, 397.2 us)
Async XLA Ops:
  7.2 61.3 %collective-permute-start.7 = (bf16[256,512]{1,0:T(8,128)(2,1)}, bf16[256,512]{1,0:T(8,128)(2,1)}, u32[]{:S(2)}, u32[]{:S(2)}) collective-permute-start(bf16[256,512]{1,0:T(8,128)(2,1)} %param.27), channel_id=1, source_target_pairs={{0,4},{4,8},{8,12},{12,16},{16,20},{20,24},{24,28},{28,0},{1,5},{5... | collective-permute-start | bytes 786440 | tf_op jit(solution)/shard_map/ppermute | solution.py:27
  7.7 66.1 %collective-permute-start.8 = (bf16[256,512]{1,0:T(8,128)(2,1)}, bf16[256,512]{1,0:T(8,128)(2,1)}, u32[]{:S(2)}, u32[]{:S(2)}) collective-permute-start(bf16[256,512]{1,0:T(8,128)(2,1)} %param.27), channel_id=1, source_target_pairs={{0,28},{4,0},{8,4},{12,8},{16,12},{20,16},{24,20},{28,24},{1,29},{... | collective-permute-start | bytes 786440 | tf_op jit(solution)/shard_map/ppermute | solution.py:32
  11.8 63.8 %collective-permute-start.14 = (bf16[256,512]{0,1:T(8,128)(2,1)}, bf16[256,512]{0,1:T(8,128)(2,1)}, u32[]{:S(2)}, u32[]{:S(2)}) collective-permute-start(bf16[256,512]{0,1:T(8,128)(2,1)} %bitcast.464), channel_id=1, source_target_pairs={{0,4},{4,8},{8,12},{12,16},{16,20},{20,24},{24,28},{28,0},{1,5},{5... | collective-permute-start | bytes 786440 | tf_op jit(solution)/shard_map/ppermute | solution.py:27
  11.8 69.0 %collective-permute-start.15 = (bf16[256,512]{0,1:T(8,128)(2,1)}, bf16[256,512]{0,1:T(8,128)(2,1)}, u32[]{:S(2)}, u32[]{:S(2)}) collective-permute-start(bf16[256,512]{0,1:T(8,128)(2,1)} %bitcast.465), channel_id=1, source_target_pairs={{0,28},{4,0},{8,4},{12,8},{16,12},{20,16},{24,20},{28,24},{1,29},{... | collective-permute-start | bytes 786440 | tf_op jit(solution)/shard_map/ppermute | solution.py:32
  15.3 43.5 %all-to-all-start = ((bf16[256,4,64]{0,2,1:T(8,128)(2,1)}), bf16[256,4,64]{0,2,1:T(8,128)(2,1)S(1)}, u32[]{:S(2)}, u32[]{:S(2)}) async-start(bf16[256,4,64]{0,2,1:T(8,128)(2,1)} %param.28), calls=%async_computation | async-start | bytes 262144 | tf_op jit(solution)/shard_map/all_to_all | solution.py:199
  63.1 798.4 %reduce-scatter.9.cloned.1.call-start = ((), (), s32[]{:S(2)}) async-start(), calls=%async_computation.11 | async-start | bytes 2359296 | tf_op jit(solution)/shard_map/reduce_scatter | solution.py:216
  111.0 59.2 %collective-permute-start.36 = (bf16[256,2048]{1,0:T(8,128)(2,1)}, bf16[256,2048]{1,0:T(8,128)(2,1)}, u32[]{:S(2)}, u32[]{:S(2)}) collective-permute-start(bf16[256,2048]{1,0:T(8,128)(2,1)} %param.33), channel_id=1, source_target_pairs={{0,4},{4,8},{8,12},{12,16},{16,20},{20,24},{24,28},{28,0},{1,5},{5... | collective-permute-start | bytes 3145736 | tf_op jit(solution)/shard_map/ppermute | solution.py:27
  112.8 62.4 %collective-permute-start.37 = (bf16[256,2048]{1,0:T(8,128)(2,1)}, bf16[256,2048]{1,0:T(8,128)(2,1)}, u32[]{:S(2)}, u32[]{:S(2)}) collective-permute-start(bf16[256,2048]{1,0:T(8,128)(2,1)} %param.33), channel_id=1, source_target_pairs={{0,28},{4,0},{8,4},{12,8},{16,12},{20,16},{24,20},{28,24},{1,29},{... | collective-permute-start | bytes 3145736 | tf_op jit(solution)/shard_map/ppermute | solution.py:32
  117.1 71.5 %collective-permute-start.29 = (bf16[256,2048]{1,0:T(8,128)(2,1)}, bf16[256,2048]{1,0:T(8,128)(2,1)}, u32[]{:S(2)}, u32[]{:S(2)}) collective-permute-start(bf16[256,2048]{1,0:T(8,128)(2,1)} %param.32), channel_id=1, source_target_pairs={{0,4},{4,8},{8,12},{12,16},{16,20},{20,24},{24,28},{28,0},{1,5},{5... | collective-permute-start | bytes 3145736 | tf_op jit(solution)/shard_map/ppermute | solution.py:27
  117.1 73.8 %collective-permute-start.30 = (bf16[256,2048]{1,0:T(8,128)(2,1)}, bf16[256,2048]{1,0:T(8,128)(2,1)}, u32[]{:S(2)}, u32[]{:S(2)}) collective-permute-start(bf16[256,2048]{1,0:T(8,128)(2,1)} %param.32), channel_id=1, source_target_pairs={{0,28},{4,0},{8,4},{12,8},{16,12},{20,16},{24,20},{28,24},{1,29},{... | collective-permute-start | bytes 3145736 | tf_op jit(solution)/shard_map/ppermute | solution.py:32
  120.7 42.1 %collective-permute-start.13 = (bf16[256,512]{1,0:T(8,128)(2,1)}, bf16[256,512]{1,0:T(8,128)(2,1)S(1)}, u32[]{:S(2)}, u32[]{:S(2)}) collective-permute-start(bf16[256,512]{1,0:T(8,128)(2,1)} %copy-done.69), channel_id=1, source_target_pairs={{0,4},{4,8},{8,12},{12,16},{16,20},{20,24},{24,28},{28,0},{1,5},{5... | collective-permute-start | bytes 786440 | tf_op jit(solution)/shard_map/ppermute | solution.py:27
  162.7 35.4 %collective-permute-start.43 = (bf16[256,2048]{0,1:T(8,128)(2,1)}, bf16[256,2048]{0,1:T(8,128)(2,1)}, u32[]{:S(2)}, u32[]{:S(2)}) collective-permute-start(bf16[256,2048]{0,1:T(8,128)(2,1)} %bitcast.43), channel_id=1, source_target_pairs={{0,4},{4,8},{8,12},{12,16},{16,20},{20,24},{24,28},{28,0},{1,5},{5... | collective-permute-start | bytes 3145736 | tf_op jit(solution)/shard_map/ppermute | solution.py:27
  170.2 35.7 %collective-permute-start.44 = (bf16[256,2048]{0,1:T(8,128)(2,1)}, bf16[256,2048]{0,1:T(8,128)(2,1)}, u32[]{:S(2)}, u32[]{:S(2)}) collective-permute-start(bf16[256,2048]{0,1:T(8,128)(2,1)} %bitcast.43), channel_id=1, source_target_pairs={{0,28},{4,0},{8,4},{12,8},{16,12},{20,16},{24,20},{28,24},{1,29},{... | collective-permute-start | bytes 3145736 | tf_op jit(solution)/shard_map/ppermute | solution.py:32
  175.3 28.9 %collective-permute-start.20 = (bf16[256,512]{0,1:T(8,128)(2,1)}, bf16[256,512]{0,1:T(8,128)(2,1)}, u32[]{:S(2)}, u32[]{:S(2)}) collective-permute-start(bf16[256,512]{0,1:T(8,128)(2,1)} %copy-done.66), channel_id=1, source_target_pairs={{0,4},{4,8},{8,12},{12,16},{16,20},{20,24},{24,28},{28,0},{1,5},{5... | collective-permute-start | bytes 786440 | tf_op jit(solution)/shard_map/ppermute | solution.py:27
  198.2 49.5 %collective-permute-start.38 = (bf16[256,2048]{1,0:T(8,128)(2,1)}, bf16[256,2048]{1,0:T(8,128)(2,1)}, u32[]{:S(2)}, u32[]{:S(2)}) collective-permute-start(bf16[256,2048]{1,0:T(8,128)(2,1)} %collective-permute-done.36), channel_id=1, source_target_pairs={{0,4},{4,8},{8,12},{12,16},{16,20},{20,24},{24,28},{28,0},{1,5},{5... | collective-permute-start | bytes 3145736 | tf_op jit(solution)/shard_map/ppermute | solution.py:27
  198.2 51.1 %collective-permute-start.39 = (bf16[256,2048]{1,0:T(8,128)(2,1)}, bf16[256,2048]{1,0:T(8,128)(2,1)}, u32[]{:S(2)}, u32[]{:S(2)}) collective-permute-start(bf16[256,2048]{1,0:T(8,128)(2,1)} %collective-permute-done.37), channel_id=1, source_target_pairs={{0,28},{4,0},{8,4},{12,8},{16,12},{20,16},{24,20},{28,24},{1,29},{... | collective-permute-start | bytes 3145736 | tf_op jit(solution)/shard_map/ppermute | solution.py:32
  204.2 49.1 %collective-permute-start.31 = (bf16[256,2048]{1,0:T(8,128)(2,1)}, bf16[256,2048]{1,0:T(8,128)(2,1)}, u32[]{:S(2)}, u32[]{:S(2)}) collective-permute-start(bf16[256,2048]{1,0:T(8,128)(2,1)} %collective-permute-done.29), channel_id=1, source_target_pairs={{0,4},{4,8},{8,12},{12,16},{16,20},{20,24},{24,28},{28,0},{1,5},{5... | collective-permute-start | bytes 3145736 | tf_op jit(solution)/shard_map/ppermute | solution.py:27
  205.9 52.2 %collective-permute-start.32 = (bf16[256,2048]{1,0:T(8,128)(2,1)}, bf16[256,2048]{1,0:T(8,128)(2,1)}, u32[]{:S(2)}, u32[]{:S(2)}) collective-permute-start(bf16[256,2048]{1,0:T(8,128)(2,1)} %collective-permute-done.30), channel_id=1, source_target_pairs={{0,28},{4,0},{8,4},{12,8},{16,12},{20,16},{24,20},{28,24},{1,29},{... | collective-permute-start | bytes 3145736 | tf_op jit(solution)/shard_map/ppermute | solution.py:32
  234.3 27.5 %collective-permute-start.21 = (bf16[512,1024]{1,0:T(8,128)(2,1)}, bf16[512,1024]{1,0:T(8,128)(2,1)}, u32[]{:S(2)}, u32[]{:S(2)}) collective-permute-start(bf16[512,1024]{1,0:T(8,128)(2,1)} %convolution_convert_fusion.6), channel_id=1, source_target_pairs={{0,1},{1,0},{2,3},{3,2},{4,5},{5,4},{6,7},{7,6},{8,9},{9,8},{10,11... | collective-permute-start | bytes 3145736 | tf_op jit(solution)/shard_map/ppermute | solution.py:107
  247.7 27.9 %collective-permute-start.45 = (bf16[256,2048]{0,1:T(8,128)(2,1)}, bf16[256,2048]{0,1:T(8,128)(2,1)}, u32[]{:S(2)}, u32[]{:S(2)}) collective-permute-start(bf16[256,2048]{0,1:T(8,128)(2,1)} %collective-permute-done.43), channel_id=1, source_target_pairs={{0,4},{4,8},{8,12},{12,16},{16,20},{20,24},{24,28},{28,0},{1,5},{5... | collective-permute-start | bytes 3145736 | tf_op jit(solution)/shard_map/ppermute | solution.py:27
  253.3 26.3 %collective-permute-start.46 = (bf16[256,2048]{0,1:T(8,128)(2,1)}, bf16[256,2048]{0,1:T(8,128)(2,1)}, u32[]{:S(2)}, u32[]{:S(2)}) collective-permute-start(bf16[256,2048]{0,1:T(8,128)(2,1)} %collective-permute-done.44), channel_id=1, source_target_pairs={{0,28},{4,0},{8,4},{12,8},{16,12},{20,16},{24,20},{28,24},{1,29},{... | collective-permute-start | bytes 3145736 | tf_op jit(solution)/shard_map/ppermute | solution.py:32
  261.9 31.9 %collective-permute-start.40 = (bf16[256,2048]{1,0:T(8,128)(2,1)}, bf16[256,2048]{1,0:T(8,128)(2,1)}, u32[]{:S(2)}, u32[]{:S(2)}) collective-permute-start(bf16[256,2048]{1,0:T(8,128)(2,1)} %collective-permute-done.38), channel_id=1, source_target_pairs={{0,4},{4,8},{8,12},{12,16},{16,20},{20,24},{24,28},{28,0},{1,5},{5... | collective-permute-start | bytes 3145736 | tf_op jit(solution)/shard_map/ppermute | solution.py:27
  261.9 39.2 %collective-permute-start.41 = (bf16[256,2048]{1,0:T(8,128)(2,1)}, bf16[256,2048]{1,0:T(8,128)(2,1)}, u32[]{:S(2)}, u32[]{:S(2)}) collective-permute-start(bf16[256,2048]{1,0:T(8,128)(2,1)} %collective-permute-done.39), channel_id=1, source_target_pairs={{0,28},{4,0},{8,4},{12,8},{16,12},{20,16},{24,20},{28,24},{1,29},{... | collective-permute-start | bytes 3145736 | tf_op jit(solution)/shard_map/ppermute | solution.py:32
  279.7 68.9 %collective-permute-start.47 = (bf16[256,2048]{0,1:T(8,128)(2,1)}, bf16[256,2048]{0,1:T(8,128)(2,1)}, u32[]{:S(2)}, u32[]{:S(2)}) collective-permute-start(bf16[256,2048]{0,1:T(8,128)(2,1)} %collective-permute-done.45), channel_id=1, source_target_pairs={{0,4},{4,8},{8,12},{12,16},{16,20},{20,24},{24,28},{28,0},{1,5},{5... | collective-permute-start | bytes 3145736 | tf_op jit(solution)/shard_map/ppermute | solution.py:27
  282.5 56.2 %collective-permute-start.33 = (bf16[256,2048]{1,0:T(8,128)(2,1)}, bf16[256,2048]{1,0:T(8,128)(2,1)}, u32[]{:S(2)}, u32[]{:S(2)}) collective-permute-start(bf16[256,2048]{1,0:T(8,128)(2,1)} %collective-permute-done.31), channel_id=1, source_target_pairs={{0,4},{4,8},{8,12},{12,16},{16,20},{20,24},{24,28},{28,0},{1,5},{5... | collective-permute-start | bytes 3145736 | tf_op jit(solution)/shard_map/ppermute | solution.py:27
  284.9 56.7 %collective-permute-start.34 = (bf16[256,2048]{1,0:T(8,128)(2,1)}, bf16[256,2048]{1,0:T(8,128)(2,1)}, u32[]{:S(2)}, u32[]{:S(2)}) collective-permute-start(bf16[256,2048]{1,0:T(8,128)(2,1)} %collective-permute-done.32), channel_id=1, source_target_pairs={{0,28},{4,0},{8,4},{12,8},{16,12},{20,16},{24,20},{28,24},{1,29},{... | collective-permute-start | bytes 3145736 | tf_op jit(solution)/shard_map/ppermute | solution.py:32
  293.8 57.4 %collective-permute-start.48 = (bf16[256,2048]{0,1:T(8,128)(2,1)}, bf16[256,2048]{0,1:T(8,128)(2,1)}, u32[]{:S(2)}, u32[]{:S(2)}) collective-permute-start(bf16[256,2048]{0,1:T(8,128)(2,1)} %collective-permute-done.46), channel_id=1, source_target_pairs={{0,28},{4,0},{8,4},{12,8},{16,12},{20,16},{24,20},{28,24},{1,29},{... | collective-permute-start | bytes 3145736 | tf_op jit(solution)/shard_map/ppermute | solution.py:32
  301.0 52.5 %collective-permute-start.25 = (bf16[256,1024]{1,0:T(8,128)(2,1)}, bf16[256,1024]{1,0:T(8,128)(2,1)}, u32[]{:S(2)}, u32[]{:S(2)}) collective-permute-start(bf16[256,1024]{1,0:T(8,128)(2,1)} %get-tuple-element.188), channel_id=1, source_target_pairs={{0,2},{2,0},{1,3},{3,1},{4,6},{6,4},{5,7},{7,5},{8,10},{10,8},{9,1... | collective-permute-start | bytes 1572872 | tf_op jit(solution)/shard_map/ppermute | solution.py:131
  348.6 38.8 %collective-permute-start.42 = (bf16[256,2048]{1,0:T(8,128)(2,1)}, bf16[256,2048]{1,0:T(8,128)(2,1)}, u32[]{:S(2)}, u32[]{:S(2)}) collective-permute-start(bf16[256,2048]{1,0:T(8,128)(2,1)} %collective-permute-done.40), channel_id=1, source_target_pairs={{0,4},{4,8},{8,12},{12,16},{16,20},{20,24},{24,28},{28,0},{1,5},{5... | collective-permute-start | bytes 3145736 | tf_op jit(solution)/shard_map/ppermute | solution.py:27
  348.6 27.5 %collective-permute-start.49 = (bf16[256,2048]{0,1:T(8,128)(2,1)}, bf16[256,2048]{0,1:T(8,128)(2,1)S(1)}, u32[]{:S(2)}, u32[]{:S(2)}) collective-permute-start(bf16[256,2048]{0,1:T(8,128)(2,1)} %collective-permute-done.47), channel_id=1, source_target_pairs={{0,4},{4,8},{8,12},{12,16},{16,20},{20,24},{24,28},{28,0},{1,5},{5... | collective-permute-start | bytes 3145736 | tf_op jit(solution)/shard_map/ppermute | solution.py:27
  351.2 37.7 %collective-permute-start.35 = (bf16[256,2048]{1,0:T(8,128)(2,1)}, bf16[256,2048]{1,0:T(8,128)(2,1)}, u32[]{:S(2)}, u32[]{:S(2)}) collective-permute-start(bf16[256,2048]{1,0:T(8,128)(2,1)} %collective-permute-done.33), channel_id=1, source_target_pairs={{0,4},{4,8},{8,12},{12,16},{16,20},{20,24},{24,28},{28,0},{1,5},{5... | collective-permute-start | bytes 3145736 | tf_op jit(solution)/shard_map/ppermute | solution.py:27
  356.2 37.8 %collective-permute-start.26 = (bf16[2,256,1024]{2,1,0:T(8,128)(2,1)}, bf16[2,256,1024]{2,1,0:T(8,128)(2,1)}, u32[]{:S(2)}, u32[]{:S(2)}) collective-permute-start(bf16[2,256,1024]{2,1,0:T(8,128)(2,1)} %pad_maximum_fusion.18), channel_id=1, source_target_pairs={{0,1},{1,0},{2,3},{3,2},{4,5},{5,4},{6,7},{7,6},{8,9},{9,8},{10,11... | collective-permute-start | bytes 3145736 | tf_op jit(solution)/shard_map/ppermute | solution.py:135
  358.6 37.1 %collective-permute-start.28 = (bf16[2,256,1024]{2,1,0:T(8,128)(2,1)}, bf16[2,256,1024]{2,1,0:T(8,128)(2,1)}, u32[]{:S(2)}, u32[]{:S(2)}) collective-permute-start(bf16[2,256,1024]{2,1,0:T(8,128)(2,1)} %pad_maximum_fusion.19), channel_id=1, source_target_pairs={{0,2},{2,0},{1,3},{3,1},{4,6},{6,4},{5,7},{7,5},{8,10},{10,8},{9,1... | collective-permute-start | bytes 3145736 | tf_op jit(solution)/shard_map/ppermute | solution.py:136
  448.4 39.7 %collective-permute-start.50 = (bf16[512,1024]{1,0:T(8,128)(2,1)}, bf16[512,1024]{1,0:T(8,128)(2,1)}, u32[]{:S(2)}, u32[]{:S(2)}) collective-permute-start(bf16[512,1024]{1,0:T(8,128)(2,1)} %fusion.98), channel_id=1, source_target_pairs={{0,1},{1,0},{2,3},{3,2},{4,5},{5,4},{6,7},{7,6},{8,9},{9,8},{10,11... | collective-permute-start | bytes 3145736 | tf_op jit(solution)/shard_map/ppermute | solution.py:107
  453.2 59.3 %collective-permute-start.52 = (bf16[512,1024]{1,0:T(8,128)(2,1)}, bf16[512,1024]{1,0:T(8,128)(2,1)S(1)}, u32[]{:S(2)}, u32[]{:S(2)}) collective-permute-start(bf16[512,1024]{1,0:T(8,128)(2,1)} %fusion.92), channel_id=1, source_target_pairs={{0,2},{2,0},{1,3},{3,1},{4,6},{6,4},{5,7},{7,5},{8,10},{10,8},{9,1... | collective-permute-start | bytes 3145736 | tf_op jit(solution)/shard_map/ppermute | solution.py:108
  491.9 36.8 %collective-permute-start.51 = (bf16[256,1024]{1,0:T(8,128)(2,1)S(1)}, bf16[256,1024]{1,0:T(8,128)(2,1)S(1)}, u32[]{:S(2)}, u32[]{:S(2)}) collective-permute-start(bf16[256,1024]{1,0:T(8,128)(2,1)S(1)} %fusion.163), channel_id=1, source_target_pairs={{0,2},{2,0},{1,3},{3,1},{4,6},{6,4},{5,7},{7,5},{8,10},{10,8},{9,1... | collective-permute-start | bytes 1572872 | tf_op jit(solution)/shard_map/ppermute | solution.py:111
  493.3 33.9 %collective-permute-start.59 = (bf16[256,1024]{1,0:T(8,128)(2,1)S(1)}, bf16[256,1024]{1,0:T(8,128)(2,1)S(1)}, u32[]{:S(2)}, u32[]{:S(2)}) collective-permute-start(bf16[256,1024]{1,0:T(8,128)(2,1)S(1)} %fusion.165), channel_id=1, source_target_pairs={{0,2},{2,0},{1,3},{3,1},{4,6},{6,4},{5,7},{7,5},{8,10},{10,8},{9,1... | collective-permute-start | bytes 1572872 | tf_op jit(solution)/shard_map/ppermute | solution.py:111
  604.1 273.6 %reduce-scatter.11.cloned.1.call-start = ((), (), s32[]{:S(2)}) async-start(), calls=%async_computation.12 | async-start | bytes 2359296 | tf_op jit(solution)/shard_map/reduce_scatter | solution.py:216
  611.3 268.4 %reduce-scatter.7.cloned.1.call-start = ((), (), s32[]{:S(2)}) async-start(), calls=%async_computation.10 | async-start | bytes 2359296 | tf_op jit(solution)/shard_map/reduce_scatter | solution.py:216
  635.0 248.5 %reduce-scatter.17.cloned.1.call-start = ((), (), s32[]{:S(2)}) async-start(), calls=%async_computation.15 | async-start | bytes 9437184 | tf_op jit(solution)/shard_map/reduce_scatter | solution.py:216
  649.2 250.6 %reduce-scatter.15.cloned.1.call-start = ((), (), s32[]{:S(2)}) async-start(), calls=%async_computation.14 | async-start | bytes 9437184 | tf_op jit(solution)/shard_map/reduce_scatter | solution.py:216
  663.9 326.1 %reduce-scatter.13.cloned.1.call-start = ((), (), s32[]{:S(2)}) async-start(), calls=%async_computation.13 | async-start | bytes 9437184 | tf_op jit(solution)/shard_map/reduce_scatter | solution.py:216
  704.6 25.2 %collective-permute-start.66 = (bf16[512,1024]{1,0:T(8,128)(2,1)}, bf16[512,1024]{1,0:T(8,128)(2,1)}, u32[]{:S(2)}, u32[]{:S(2)}) collective-permute-start(bf16[512,1024]{1,0:T(8,128)(2,1)} %add_convert_fusion.1), channel_id=1, source_target_pairs={{0,1},{1,0},{2,3},{3,2},{4,5},{5,4},{6,7},{7,6},{8,9},{9,8},{10,11... | collective-permute-start | bytes 3145736 | tf_op jit(solution)/shard_map/ppermute | solution.py:107
  723.8 26.3 %collective-permute-start.68 = (bf16[512,1024]{1,0:T(8,128)(2,1)}, bf16[512,1024]{1,0:T(8,128)(2,1)S(1)}, u32[]{:S(2)}, u32[]{:S(2)}) collective-permute-start(bf16[512,1024]{1,0:T(8,128)(2,1)} %add_convert_fusion), channel_id=1, source_target_pairs={{0,2},{2,0},{1,3},{3,1},{4,6},{6,4},{5,7},{7,5},{8,10},{10,8},{9,1... | collective-permute-start | bytes 3145736 | tf_op jit(solution)/shard_map/ppermute | solution.py:108
  731.9 28.5 %collective-permute-start.67 = (bf16[256,1024]{1,0:T(8,128)(2,1)S(1)}, bf16[256,1024]{1,0:T(8,128)(2,1)S(1)}, u32[]{:S(2)}, u32[]{:S(2)}) collective-permute-start(bf16[256,1024]{1,0:T(8,128)(2,1)S(1)} %fusion.167), channel_id=1, source_target_pairs={{0,2},{2,0},{1,3},{3,1},{4,6},{6,4},{5,7},{7,5},{8,10},{10,8},{9,1... | collective-permute-start | bytes 1572872 | tf_op jit(solution)/shard_map/ppermute | solution.py:111
  753.6 24.9 %collective-permute-start.55 = (bf16[2,256,1024]{2,1,0:T(8,128)(2,1)}, bf16[2,256,1024]{2,1,0:T(8,128)(2,1)}, u32[]{:S(2)}, u32[]{:S(2)}) collective-permute-start(bf16[2,256,1024]{2,1,0:T(8,128)(2,1)} %pad_maximum_fusion.20), channel_id=1, source_target_pairs={{0,1},{1,0},{2,3},{3,2},{4,5},{5,4},{6,7},{7,6},{8,9},{9,8},{10,11... | collective-permute-start | bytes 3145736 | tf_op jit(solution)/shard_map/ppermute | solution.py:135
  790.9 67.1 %collective-permute-start.71 = (bf16[2,256,1024]{2,1,0:T(8,128)(2,1)}, bf16[2,256,1024]{2,1,0:T(8,128)(2,1)S(1)}, u32[]{:S(2)}, u32[]{:S(2)}) collective-permute-start(bf16[2,256,1024]{2,1,0:T(8,128)(2,1)} %pad_maximum_fusion.26), channel_id=1, source_target_pairs={{0,1},{1,0},{2,3},{3,2},{4,5},{5,4},{6,7},{7,6},{8,9},{9,8},{10,11... | collective-permute-start | bytes 3145736 | tf_op jit(solution)/shard_map/ppermute | solution.py:135
  794.0 64.6 %collective-permute-start.73 = (bf16[2,256,1024]{2,1,0:T(8,128)(2,1)}, bf16[2,256,1024]{2,1,0:T(8,128)(2,1)}, u32[]{:S(2)}, u32[]{:S(2)}) collective-permute-start(bf16[2,256,1024]{2,1,0:T(8,128)(2,1)} %pad_maximum_fusion.27), channel_id=1, source_target_pairs={{0,2},{2,0},{1,3},{3,1},{4,6},{6,4},{5,7},{7,5},{8,10},{10,8},{9,1... | collective-permute-start | bytes 3145736 | tf_op jit(solution)/shard_map/ppermute | solution.py:136
  (131 other events, 1533.1 us)
Sparse Core Ops, SparseCore 0:
  604.3 40.3 reduce-scatter.8
  646.9 34.4 reduce-scatter.10
  683.7 34.4 reduce-scatter.6
  720.3 88.2 reduce-scatter.16
  810.8 89.0 reduce-scatter.14
  902.0 87.9 reduce-scatter.12
